TPU v7x, 32 devices: a whole 2x2x4 slice. The times are simulated.
32 devices in a mesh: row: 4 (over y, core), col: 8 (over z, x).
Axes of the slice: x: 2, y: 2, z: 4, core: 2. Of those that a mesh axis runs over, the one named last changes fastest.
Arguments:
- tokens: bfloat16 [3072, 6144], P('row'), may hold values from -6 to 6
- routes: int32 [3072, 2], P('row'), may hold values from 0 to 7, as said below
- w_master: float32 [6144, 2, 9216], P('row', None, 'col'), may hold values from -1 to 1
- d_hidden: bfloat16 [768, 9216], P('row', 'col'), may hold values from -6 to 6
Outputs:
- hidden: bfloat16 [768, 9216], P('row', 'col')
- update: float32 [6144, 2, 9216], P('row', None, 'col')
- new_master: float32 [6144, 2, 9216], P('row', None, 'col')
Inputs may be any that keep to these rules, and one draw needn't show every extreme that they name: `routes`: in every aligned block of 768 tokens exactly 192 tokens name expert 0; the two experts of a token differ; every expert is named.
All inputs are finite; a program needn't handle non-finite values. Where the computation divides by a largest or mean magnitude, that divisor is 1e-20 or more.
Results may differ from a plain program's by a relative error of at most 0.023.
Values may be sent and summed in bfloat16 or wider, within the bound.
A program may use at most 128 MiB of HBM per device.

v0:
```python
import jax
import jax.numpy as jnp
from jax import lax
from jax.experimental import pallas as pl
from jax.experimental.pallas import tpu as pltpu
from jax.sharding import PartitionSpec as P

BLK = 128


epsilon = 1e-06
quant_range = 448.0
learn_rate = 0.05


def on_device_plain(tokens, routes, w_master, d_hidden):
    rows_local, _, columns = w_master.shape
    slots = d_hidden.shape[0]
    colmax = lax.pmax(jnp.max(jnp.abs(w_master), axis=0), "row")
    wscale = (colmax + epsilon) / quant_range
    quantized = (w_master / wscale).astype(jnp.bfloat16).reshape(rows_local, 2 * columns)
    flat_scale = wscale.reshape(2 * columns)
    routed = jnp.any(routes == 0, axis=1)
    picked = jnp.nonzero(routed, size=slots)[0].astype(jnp.int32)
    slot_rows = tokens[picked]
    slot_cols = lax.all_to_all(slot_rows, "row", split_axis=1, concat_axis=0, tiled=True)
    slot_part = lax.slice_in_dim(slot_cols, 0, lax.axis_size("row") * slots, axis=0)
    summed = lax.psum_scatter(
        jnp.dot(slot_part, quantized, preferred_element_type=jnp.float32).astype(jnp.bfloat16),
        "row",
        scatter_dimension=0,
        tiled=True,
    ).astype(jnp.float32)
    projected = (summed * flat_scale).reshape(slots, 2, columns)
    gate_pre = projected[:, 0]
    up_pre = projected[:, 1]
    gate_sig = jax.nn.sigmoid(gate_pre)
    gate_act = gate_pre * gate_sig
    hidden = (gate_act * up_pre).astype(jnp.bfloat16)
    upstream = d_hidden.astype(jnp.float32)
    grad_gate = upstream * up_pre * gate_sig * (1.0 + gate_pre * (1.0 - gate_sig))
    grad_up = upstream * gate_act
    grad_pre = (
        jnp.stack([grad_gate, grad_up], axis=1).astype(jnp.bfloat16).reshape(slots, 2 * columns)
    )
    shard_piece = lax.all_gather(grad_pre, "row", axis=0, tiled=True)
    groups = shard_piece.shape[0] // slots
    slot_part = lax.slice_in_dim(slot_cols, 0, shard_piece.shape[0], axis=0).reshape(
        groups, slots, rows_local
    )
    block_terms = jnp.einsum(
        "gsd,gsf->gdf",
        slot_part,
        shard_piece.reshape(groups, slots, 2 * columns),
        preferred_element_type=jnp.float32,
    )
    rounded = lax.optimization_barrier(block_terms.astype(jnp.bfloat16)).astype(jnp.float32)
    grad_full = jnp.sum(rounded, axis=0)
    grad_blocks = grad_full.reshape(rows_local // BLK, BLK, 2, columns)
    block_max = lax.pmax(jnp.max(jnp.abs(grad_blocks), axis=(1, 3)), "col")
    update = (grad_blocks / (block_max[:, None, :, None] + epsilon)).reshape(rows_local, 2, columns)
    new_master = w_master - learn_rate * colmax * update
    return (hidden, update, new_master)


LANE = 128
SUB = 8


def moved(src, dst, send, recv, to):
    return pltpu.make_async_remote_copy(
        src_ref=src,
        dst_ref=dst,
        send_sem=send,
        recv_sem=recv,
        device_id={"row": to},
        device_id_type=pl.DeviceIdType.MESH,
    )


def forward_kernel(
    mask_ref, dh_ref, tok_hbm, w_hbm, hid_ref, sc_ref, ga_ref, cm_ref,
    tokv, asend, wv, folded, cmx, psend, prec, keep, own, xsend, xrec,
    tok_sem, w_sem, a_send, a_recv, c_send, c_recv, p_send, p_recv,
    x_send, x_recv, ga_send, ga_recv, gp_send, gp_recv, gf_send, gf_recv,
):
    me = lax.axis_index("row")
    core = lax.rem(me, 2)
    partner = me + 1 - 2 * core
    across = lax.rem(me + 2, 4)
    diag = lax.rem(partner + 2, 4)
    where_to = (me, across, partner, diag)
    tiles = ga_ref.shape[0]
    slots = hid_ref.shape[0]
    rows = sc_ref.shape[1]
    toks = mask_ref.shape[1]
    chunks = w_sem.shape[1]
    piece = rows // chunks

    order = (3, 1, 2, 0)
    tok_copies = {}
    for j in order:
        cols = pl.ds(pl.multiple_of(where_to[j] * rows, LANE), rows)
        tok_copies[j] = pltpu.make_async_copy(tok_hbm.at[:, cols], tokv.at[j], tok_sem.at[j])
        tok_copies[j].start()
    w_copies = []
    for k in range(chunks):
        part = pl.ds(k * piece, piece)
        for p in range(2):
            w_copies.append(
                pltpu.make_async_copy(w_hbm.at[part, p, :], wv.at[p, part], w_sem.at[p, k])
            )
            w_copies[-1].start()

    barrier = pltpu.get_barrier_semaphore()
    for j in (1, 2, 3):
        pl.semaphore_signal(
            barrier, inc=1, device_id={"row": where_to[j]}, device_id_type=pl.DeviceIdType.MESH
        )

    mask = mask_ref[...]
    before = lax.broadcasted_iota(jnp.int32, (toks, toks), 0)
    after = lax.broadcasted_iota(jnp.int32, (toks, toks), 1)
    ladder = jnp.where(before < after, 1.0, 0.0).astype(jnp.bfloat16)
    place = jnp.dot(mask, ladder, preferred_element_type=jnp.float32)[0:1, :].astype(jnp.int32)
    flag = mask[0:1, :].astype(jnp.float32)
    slot_id = lax.broadcasted_iota(jnp.int32, (slots, toks), 0)
    pick = jnp.where(slot_id == place, flag, 0.0).astype(jnp.bfloat16)
    pl.semaphore_wait(barrier, 3)

    a_copies = {}
    for j in order:
        tok_copies[j].wait()
        got = jnp.dot(pick, tokv[j], preferred_element_type=jnp.float32).astype(jnp.bfloat16)
        if j == 0:
            sc_ref[0:slots, :] = got
        else:
            asend[j - 1] = got
            a_copies[j] = moved(
                asend.at[j - 1],
                sc_ref.at[pl.ds(j * slots, slots)],
                a_send.at[j - 1],
                a_recv.at[j - 1],
                where_to[j],
            )
            a_copies[j].start()

    folded[...] = jnp.zeros(folded.shape, jnp.float32)
    for k in range(chunks):
        for p in range(2):
            w_copies[2 * k + p].wait()

        def fold(t, carry, k=k):
            cols = pl.ds(pl.multiple_of(t * LANE, LANE), LANE)
            for p in range(2):
                tile = jnp.abs(wv[p, k * piece : (k + 1) * piece, cols])
                best = jnp.max(tile.reshape(-1, SUB, LANE), axis=0)
                folded[p, :, cols] = jnp.maximum(folded[p, :, cols], best)
            return carry

        lax.fori_loop(0, tiles, fold, 0)
    cmx[0] = jnp.zeros(cmx.shape[1:], jnp.float32)
    for p in range(2):
        cmx[0, p : p + 1, :] = jnp.max(folded[p], axis=0, keepdims=True)
    c_copies = []
    for j in (1, 2, 3):
        c_copies.append(moved(cmx.at[0], cmx.at[j], c_send.at[j - 1], c_recv.at[j - 1], where_to[j]))
        c_copies[-1].start()
    for copy in c_copies:
        copy.wait()
    cm_ref[...] = jnp.maximum(jnp.maximum(cmx[0], cmx[1]), jnp.maximum(cmx[2], cmx[3]))
    for j in (3, 1, 2):
        a_copies[j].wait()

    def scale_row(t, p):
        cols = pl.ds(pl.multiple_of(t * LANE, LANE), LANE)
        return (cm_ref[p : p + 1, cols] + epsilon) / quant_range

    def swap(t):
        return moved(psend.at[t], prec.at[t], p_send.at[t], p_recv.at[t], partner)

    def cross(t):
        return moved(xsend.at[t], xrec.at[t], x_send.at[t], x_recv.at[t], across)

    def grad_block(t, j):
        return ga_ref.at[t, pl.ds(j * slots, slots)]

    def share_across(t):
        return moved(grad_block(t, 0), grad_block(t, 1), ga_send.at[t], ga_recv.at[t], across)

    def share_partner(t):
        return moved(grad_block(t, 0), grad_block(t, 2), gp_send.at[t], gp_recv.at[t], partner)

    def forward(t):
        return moved(grad_block(t, 1), grad_block(t, 3), gf_send.at[t], gf_recv.at[t], partner)

    def step(i, carry):
        @pl.when(i < tiles)
        def _():
            t = i
            halves = []
            for p in range(2):
                w = wv[p, :, pl.ds(pl.multiple_of(t * LANE, LANE), LANE)]
                halves.append((w * (1.0 / scale_row(t, p))).astype(jnp.bfloat16))
            quantized = jnp.concatenate(halves, axis=1)
            term = jnp.dot(sc_ref[...], quantized, preferred_element_type=jnp.float32)
            slot = lax.rem(t, 2)
            psend[t] = term[2 * slots :].astype(jnp.bfloat16)
            keep[slot] = term[: 2 * slots]
            swap(t).start()

        @pl.when(jnp.logical_and(i >= 1, i < tiles + 1))
        def _():
            t = i - 1
            slot = lax.rem(t, 2)
            swap(t).wait_recv()
            own[slot] = keep[slot, :slots] + prec[t, :slots].astype(jnp.float32)
            xsend[t] = (keep[slot, slots:] + prec[t, slots:].astype(jnp.float32)).astype(jnp.bfloat16)
            cross(t).start()

        @pl.when(jnp.logical_and(i >= 2, i < tiles + 2))
        def _():
            t = i - 2
            cross(t).wait_recv()
            total = own[lax.rem(t, 2)] + xrec[t].astype(jnp.float32)
            gate_pre = total[:, :LANE] * scale_row(t, 0)
            up_pre = total[:, LANE:] * scale_row(t, 1)
            gate_sig = jax.nn.sigmoid(gate_pre)
            gate_act = gate_pre * gate_sig
            cols = pl.ds(pl.multiple_of(t * LANE, LANE), LANE)
            hid_ref[:, cols] = (gate_act * up_pre).astype(jnp.bfloat16)
            upstream = dh_ref[:, cols].astype(jnp.float32)
            grad_gate = upstream * up_pre * gate_sig * (1.0 + gate_pre * (1.0 - gate_sig))
            grad_up = upstream * gate_act
            ga_ref[t, 0:slots, :] = jnp.concatenate([grad_gate, grad_up], axis=1).astype(jnp.bfloat16)
            share_across(t).start()
            share_partner(t).start()

        @pl.when(i >= 3)
        def _():
            t = i - 3
            share_across(t).wait_recv()
            forward(t).start()

        return carry

    lax.fori_loop(0, tiles + 3, step, 0)

    def finish(t, carry):
        swap(t).wait_send()
        cross(t).wait_send()
        share_across(t).wait_send()
        share_partner(t).wait()
        forward(t).wait()
        return carry

    lax.fori_loop(0, tiles, finish, 0)


def gradient_kernel(sc_ref, ga_ref, grad_ref, top_ref, turned):
    tiles = ga_ref.shape[0]
    depth = grad_ref.shape[0]
    turned[...] = sc_ref[...].T
    blocks = depth // BLK
    tops = tuple(jnp.zeros((SUB, LANE), jnp.float32) for _ in range(2 * blocks))

    def step(t, tops):
        grad = jnp.dot(turned[...], ga_ref[t], preferred_element_type=jnp.float32)
        grad_ref[:, pl.ds(pl.multiple_of(t * 2 * LANE, 2 * LANE), 2 * LANE)] = grad.astype(jnp.bfloat16)
        out = []
        for b in range(blocks):
            for p in range(2):
                tile = jnp.abs(grad[b * BLK : (b + 1) * BLK, p * LANE : (p + 1) * LANE])
                out.append(jnp.maximum(tops[2 * b + p], jnp.max(tile.reshape(-1, SUB, LANE), axis=0)))
        return tuple(out)

    tops = lax.fori_loop(0, tiles, step, tops)
    for n in range(2 * blocks):
        top_ref[0, n] = tops[n]


def update_kernel(inv_ref, cm_ref, w_hbm, grad_hbm, update_hbm, new_hbm, wv, uv, gv, w_sem, g_sem, u_sem, n_sem):
    blocks = g_sem.shape[0]
    columns = wv.shape[2]
    tiles = columns // LANE

    def part(b):
        return pl.ds(pl.multiple_of(b * BLK, BLK), BLK)

    def old(b, p):
        return pltpu.make_async_copy(w_hbm.at[part(b), p, :], wv.at[p, part(b)], w_sem.at[p, b])

    def gradient(b):
        return pltpu.make_async_copy(grad_hbm.at[part(b)], gv.at[part(b)], g_sem.at[b])

    def put_update(b, p):
        return pltpu.make_async_copy(uv.at[p, part(b)], update_hbm.at[part(b), p, :], u_sem.at[p, b])

    def put_new(b, p):
        return pltpu.make_async_copy(wv.at[p, part(b)], new_hbm.at[part(b), p, :], n_sem.at[p, b])

    def begin(b, carry):
        gradient(b).start()
        for p in range(2):
            old(b, p).start()
        return carry

    def step(b, carry):
        gradient(b).wait()
        for p in range(2):
            old(b, p).wait()
            inverse = inv_ref[2 * b + p]
            for t in range(tiles):
                cols = slice(t * LANE, (t + 1) * LANE)
                at = (2 * t + p) * LANE
                update = gv[part(b), at : at + LANE].astype(jnp.float32) * inverse
                uv[p, part(b), cols] = update
                wv[p, part(b), cols] = wv[p, part(b), cols] - (learn_rate * cm_ref[p : p + 1, cols]) * update
            put_update(b, p).start()
            put_new(b, p).start()
        return carry

    def finish(b, carry):
        for p in range(2):
            put_update(b, p).wait()
            put_new(b, p).wait()
        return carry

    lax.fori_loop(0, blocks, begin, 0)
    lax.fori_loop(0, blocks, step, 0)
    lax.fori_loop(0, blocks, finish, 0)


def on_device(tokens, routes, w_master, d_hidden):
    rows, _, columns = w_master.shape
    slots = d_hidden.shape[0]
    toks = tokens.shape[0]
    depth = 3 * BLK
    aligned = columns % LANE == 0 and rows % depth == 0 and slots % 16 == 0 and toks % LANE == 0
    if lax.axis_size("row") != 4 or not aligned:
        return on_device_plain(tokens, routes, w_master, d_hidden)
    tiles = columns // LANE
    bf16, f32 = jnp.bfloat16, jnp.float32
    routed = jnp.any(routes == 0, axis=1).astype(bf16)
    mask = jnp.broadcast_to(routed[None, :], (16, toks))
    chunks = 6
    blocks = rows // BLK
    vmem = pl.BlockSpec(memory_space=pltpu.VMEM)
    hbm = pl.BlockSpec(memory_space=pl.ANY)
    dma = pltpu.SemaphoreType.DMA
    wide = 2 * LANE
    hidden, slot_cols, grads, colmax = pl.pallas_call(
        forward_kernel,
        name="forward_exchange",
        out_shape=(
            jax.ShapeDtypeStruct((slots, columns), bf16),
            jax.ShapeDtypeStruct((4 * slots, rows), bf16),
            jax.ShapeDtypeStruct((tiles, 4 * slots, wide), bf16),
            jax.ShapeDtypeStruct((SUB, columns), f32),
        ),
        in_specs=[vmem, vmem, hbm, hbm],
        out_specs=(vmem, vmem, vmem, vmem),
        scratch_shapes=[
            pltpu.VMEM((4, toks, rows), bf16),
            pltpu.VMEM((3, slots, rows), bf16),
            pltpu.VMEM((2, rows, columns), f32),
            pltpu.VMEM((2, SUB, columns), f32),
            pltpu.VMEM((4, SUB, columns), f32),
            pltpu.VMEM((tiles, 2 * slots, wide), bf16),
            pltpu.VMEM((tiles, 2 * slots, wide), bf16),
            pltpu.VMEM((2, 2 * slots, wide), f32),
            pltpu.VMEM((2, slots, wide), f32),
            pltpu.VMEM((tiles, slots, wide), bf16),
            pltpu.VMEM((tiles, slots, wide), bf16),
            dma((4,)),
            dma((2, chunks)),
            dma((3,)),
            dma((3,)),
            dma((3,)),
            dma((3,)),
        ]
        + [dma((tiles,))] * 10,
        compiler_params=pltpu.CompilerParams(
            collective_id=0, has_side_effects=True, vmem_limit_bytes=58 * 1024 * 1024
        ),
    )(mask, d_hidden, tokens, w_master)
    steps = rows // depth
    grad, tops = pl.pallas_call(
        gradient_kernel,
        name="weight_gradient",
        grid=(steps,),
        out_shape=(
            jax.ShapeDtypeStruct((rows, 2 * columns), bf16),
            jax.ShapeDtypeStruct((steps, 6, SUB, LANE), f32),
        ),
        in_specs=[
            pl.BlockSpec((4 * slots, depth), lambda d: (0, d)),
            pl.BlockSpec((tiles, 4 * slots, wide), lambda d: (0, 0, 0)),
        ],
        out_specs=(
            pl.BlockSpec((depth, 2 * columns), lambda d: (d, 0)),
            pl.BlockSpec((1, 6, SUB, LANE), lambda d: (d, 0, 0, 0)),
        ),
        scratch_shapes=[pltpu.VMEM((depth, 4 * slots), bf16)],
        compiler_params=pltpu.CompilerParams(vmem_limit_bytes=32 * 1024 * 1024),
    )(slot_cols, grads)
    block_max = lax.pmax(jnp.max(tops, axis=(2, 3)).reshape(-1), "col")
    inverse = 1.0 / (block_max + epsilon)
    update, new_master = pl.pallas_call(
        update_kernel,
        name="master_update",
        out_shape=(jax.ShapeDtypeStruct(w_master.shape, f32),) * 2,
        in_specs=[pl.BlockSpec(memory_space=pltpu.SMEM), vmem, hbm, hbm],
        out_specs=(hbm, hbm),
        scratch_shapes=[
            pltpu.VMEM((2, rows, columns), f32),
            pltpu.VMEM((2, rows, columns), f32),
            pltpu.VMEM((rows, 2 * columns), bf16),
            dma((2, blocks)),
            dma((blocks,)),
            dma((2, blocks)),
            dma((2, blocks)),
        ],
        compiler_params=pltpu.CompilerParams(vmem_limit_bytes=48 * 1024 * 1024),
    )(inverse, colmax, w_master, grad)
    return (hidden, update, new_master)


def solution(mesh):
    in_specs = (P("row", None), P("row", None), P("row", None, "col"), P("row", "col"))
    out_specs = (P("row", "col"), P("row", None, "col"), P("row", None, "col"))
    return jax.shard_map(
        on_device, mesh=mesh, in_specs=in_specs, out_specs=out_specs, check_vma=False
    )
```

profile of v0, /device:TPU:0, one launch (start us, length us, event | category | flops | bytes accessed | tf_op | source)
XLA Modules:
  0.0 143.6 jit_solution(8268045746803520790)
XLA Ops:
  0.6 0.7 compare_reduce_fusion
  1.4 0.6 broadcast_in_dim.2.mask_ref
  2.0 80.2 %forward_exchange.1 = (bf16[192,1152]{1,0:T(8,128)(2,1)}, bf16[768,1536]{1,0:T(8,128)(2,1)}, bf16[9,768,256]{2,1,0:T(8,128)(2,1)}, f32[8,1152]{1,0:T(8,128)}) custom-call(bf16[16,768]{1,0:T(8,128)(2,1)} %broadcast_in_dim.2.mask_ref, bf16[192,1152]{1,0:T(8,128)(2,1)} %dh_ref.1, bf16[768,6144]{1,0:T(8,128)(2,1)} %tok_hbm.1, f32[1536,2,1152]{2,1,0:T(2,128)} %w_hbm.3), custom_call_target="tpu_custom_call" | custom-call | tf_op jit(solution)/shard_map/forward_exchange/pallas_call | solution.py:352
  82.2 0.0 copy-start.1
  82.2 2.0 %copy-done.1 = bf16[9,768,256]{2,1,0:T(8,128)(2,1)S(1)} copy-done((bf16[9,768,256]{2,1,0:T(8,128)(2,1)S(1)}, bf16[9,768,256]{2,1,0:T(8,128)(2,1)}, u32[]{:S(2)}) %copy-start.1) | copy-done | bytes 3538968
  84.2 0.0 copy-start.2
  84.2 1.7 %copy-done.2 = bf16[768,1536]{1,0:T(8,128)(2,1)S(1)} copy-done((bf16[768,1536]{1,0:T(8,128)(2,1)S(1)}, bf16[768,1536]{1,0:T(8,128)(2,1)}, u32[]{:S(2)}) %copy-start.2) | copy-done | bytes 2359320
  85.8 12.8 %weight_gradient.1 = (bf16[1536,2304]{1,0:T(8,128)(2,1)S(1)}, f32[4,6,8,128]{3,2,1,0:T(8,128)S(1)}) custom-call(bf16[768,1536]{1,0:T(8,128)(2,1)S(1)} %copy-done.2, bf16[9,768,256]{2,1,0:T(8,128)(2,1)S(1)} %copy-done.1), custom_call_target="tpu_custom_call" | custom-call | tf_op jit(solution)/shard_map/weight_gradient/pallas_call | solution.py:388
  98.7 0.0 copy-start
  98.7 2.9 %copy-done = bf16[1536,2304]{1,0:T(8,128)(2,1)} copy-done((bf16[1536,2304]{1,0:T(8,128)(2,1)}, bf16[1536,2304]{1,0:T(8,128)(2,1)S(1)}, u32[]{:S(2)}) %copy-start) | copy-done | bytes 7077912
  101.6 0.1 reduce_max.9
  101.7 0.1 reshape.12
  101.8 21.6 %pmax.7 = f32[24]{0:T(128)S(1)} all-reduce(f32[24]{0:T(128)S(1)} %reshape.12), channel_id=1, replica_groups=mesh['row'=4,'col'=8] {'col'}, use_global_device_ids=true, to_apply=%region_2.0 | all-reduce | flops 24 | bytes 192 | tf_op jit(solution)/shard_map/pmax | solution.py:407
  123.4 0.0 copy-start.3
  123.4 0.8 copy-done.3
  124.2 0.0 copy-start.4
  124.2 18.6 %master_update.1 = (f32[1536,2,1152]{2,1,0:T(2,128)}, f32[1536,2,1152]{2,1,0:T(2,128)}) custom-call(f32[24]{0:T(128)S(1)} %add_divide_fusion.inv_ref, f32[8,1152]{1,0:T(8,128)S(1)} %copy-done.3, f32[1536,2,1152]{2,1,0:T(2,128)} %w_hbm.3, bf16[1536,2304]{1,0:T(8,128)(2,1)} %copy-done), custom_call_target="tpu_custom_call" | custom-call | tf_op jit(solution)/shard_map/master_update/pallas_call | solution.py:409
  142.8 0.0 copy-done.4
  142.8 0.8 copy.8
  (2 shorter events, 0.0 us)
Async XLA Ops:
  82.2 2.0 %copy-start.1 = (bf16[9,768,256]{2,1,0:T(8,128)(2,1)S(1)}, bf16[9,768,256]{2,1,0:T(8,128)(2,1)}, u32[]{:S(2)}) copy-start(bf16[9,768,256]{2,1,0:T(8,128)(2,1)} %get-tuple-element.13.ga_ref) | copy-start | bytes 10616836
  84.2 1.7 %copy-start.2 = (bf16[768,1536]{1,0:T(8,128)(2,1)S(1)}, bf16[768,1536]{1,0:T(8,128)(2,1)}, u32[]{:S(2)}) copy-start(bf16[768,1536]{1,0:T(8,128)(2,1)} %get-tuple-element.12.sc_ref) | copy-start | bytes 7077892
  98.7 2.9 %copy-start = (bf16[1536,2304]{1,0:T(8,128)(2,1)}, bf16[1536,2304]{1,0:T(8,128)(2,1)S(1)}, u32[]{:S(2)}) copy-start(bf16[1536,2304]{1,0:T(8,128)(2,1)S(1)} %get-tuple-element.16.grad_hbm) | copy-start | bytes 21233668
  123.4 0.8 copy-start.3
  124.2 18.6 %copy-start.4 = (bf16[192,1152]{1,0:T(8,128)(2,1)S(1)}, bf16[192,1152]{1,0:T(8,128)(2,1)}, u32[]{:S(2)}) copy-start(bf16[192,1152]{1,0:T(8,128)(2,1)} %get-tuple-element.22) | copy-start | bytes 1327108
where the time goes:
time: 144 us
  Pallas kernels  112 us (78%)
  blocking collectives  21.6 us (15%)
  local copies, waits for them, and re-layouts  8.81 us (6%)
    pallas_call x1, Pallas kernels, on_device(): pl.pallas_call(forward_kernel, name='forward_exchange', out_shape=(jax.Sh...  80.2 us
    pmax x1, blocking collectives, on_device(): block_max = lax.pmax(jnp.max(tops, axis=(2, 3)).reshape(-1), 'col')  21.6 us
    pallas_call x1, Pallas kernels, on_device(): pl.pallas_call(update_kernel, name='master_update', out_shape=(jax.ShapeD...  18.6 us
    pallas_call x1, Pallas kernels, on_device(): pl.pallas_call(gradient_kernel, name='weight_gradient', grid=(steps,), ou...  12.8 us
    unnamed x11, local copies, waits for them, and re-layouts  8.11 us

commit v1 on v0

v1 whole, which is shorter than its diff:
```python
import jax
import jax.numpy as jnp
from jax import lax
from jax.experimental import pallas as pl
from jax.experimental.pallas import tpu as pltpu
from jax.sharding import PartitionSpec as P

BLK = 128


epsilon = 1e-06
quant_range = 448.0
learn_rate = 0.05


def on_device_plain(tokens, routes, w_master, d_hidden):
    rows_local, _, columns = w_master.shape
    slots = d_hidden.shape[0]
    colmax = lax.pmax(jnp.max(jnp.abs(w_master), axis=0), "row")
    wscale = (colmax + epsilon) / quant_range
    quantized = (w_master / wscale).astype(jnp.bfloat16).reshape(rows_local, 2 * columns)
    flat_scale = wscale.reshape(2 * columns)
    routed = jnp.any(routes == 0, axis=1)
    picked = jnp.nonzero(routed, size=slots)[0].astype(jnp.int32)
    slot_rows = tokens[picked]
    slot_cols = lax.all_to_all(slot_rows, "row", split_axis=1, concat_axis=0, tiled=True)
    slot_part = lax.slice_in_dim(slot_cols, 0, lax.axis_size("row") * slots, axis=0)
    summed = lax.psum_scatter(
        jnp.dot(slot_part, quantized, preferred_element_type=jnp.float32).astype(jnp.bfloat16),
        "row",
        scatter_dimension=0,
        tiled=True,
    ).astype(jnp.float32)
    projected = (summed * flat_scale).reshape(slots, 2, columns)
    gate_pre = projected[:, 0]
    up_pre = projected[:, 1]
    gate_sig = jax.nn.sigmoid(gate_pre)
    gate_act = gate_pre * gate_sig
    hidden = (gate_act * up_pre).astype(jnp.bfloat16)
    upstream = d_hidden.astype(jnp.float32)
    grad_gate = upstream * up_pre * gate_sig * (1.0 + gate_pre * (1.0 - gate_sig))
    grad_up = upstream * gate_act
    grad_pre = (
        jnp.stack([grad_gate, grad_up], axis=1).astype(jnp.bfloat16).reshape(slots, 2 * columns)
    )
    shard_piece = lax.all_gather(grad_pre, "row", axis=0, tiled=True)
    groups = shard_piece.shape[0] // slots
    slot_part = lax.slice_in_dim(slot_cols, 0, shard_piece.shape[0], axis=0).reshape(
        groups, slots, rows_local
    )
    block_terms = jnp.einsum(
        "gsd,gsf->gdf",
        slot_part,
        shard_piece.reshape(groups, slots, 2 * columns),
        preferred_element_type=jnp.float32,
    )
    rounded = lax.optimization_barrier(block_terms.astype(jnp.bfloat16)).astype(jnp.float32)
    grad_full = jnp.sum(rounded, axis=0)
    grad_blocks = grad_full.reshape(rows_local // BLK, BLK, 2, columns)
    block_max = lax.pmax(jnp.max(jnp.abs(grad_blocks), axis=(1, 3)), "col")
    update = (grad_blocks / (block_max[:, None, :, None] + epsilon)).reshape(rows_local, 2, columns)
    new_master = w_master - learn_rate * colmax * update
    return (hidden, update, new_master)


LANE = 128
SUB = 8
LEAD = 3


def moved(src, dst, send, recv, to):
    return pltpu.make_async_remote_copy(
        src_ref=src,
        dst_ref=dst,
        send_sem=send,
        recv_sem=recv,
        device_id=to,
        device_id_type=pl.DeviceIdType.MESH,
    )


def flipped(index, bit):
    return index + bit - 2 * bit * lax.rem(index // bit, 2)


def layer_kernel(
    routes_hbm, dh_hbm, tok_hbm, w_hbm, hid, grad_ref, cm_ref, inv_ref, wv,
    routes, dh, tokv, tokq, psendt, qsend, sc, turned, folded, cmx,
    psend, prec, keep, own, xsend, xrec, ga, tops, bmx,
    in_sem, tok_sem, w_sem, pt_send, pt_recv, y_send, y_recv, x_send, x_recv, z_send, z_recv,
    c_send, c_recv, b_send, b_recv,
    p_send, p_recv, xs_send, xs_recv, ga_send, ga_recv, gp_send, gp_recv, gf_send, gf_recv,
):
    me = lax.axis_index("row")
    col = lax.axis_index("col")
    core = lax.rem(me, 2)
    partner = me + 1 - 2 * core
    across = lax.rem(me + 2, 4)
    diag = lax.rem(partner + 2, 4)
    where_to = (me, across, partner, diag)
    group = bmx.shape[0]
    col_x = flipped(col, 1)
    col_z = flipped(col, 2)
    col_far = flipped(col, 4)
    quarter_of = lax.rem(col, 4)
    quarter_x = lax.rem(col_x, 4)
    quarter_z = lax.rem(col_z, 4)
    tiles = ga.shape[0]
    slots = hid.shape[0]
    rows = sc.shape[1]
    toks = routes.shape[1]
    chunks = w_sem.shape[1]
    piece = rows // chunks
    quarter = rows // 4
    half = slots // 2

    in_copies = (
        pltpu.make_async_copy(routes_hbm, routes, in_sem.at[0]),
        pltpu.make_async_copy(dh_hbm, dh, in_sem.at[1]),
    )
    in_copies[0].start()
    q_copies = {}
    for n, j in enumerate((1, 3)):
        cols = pl.ds(pl.multiple_of(where_to[j] * rows + quarter_of * quarter, LANE), quarter)
        q_copies[n] = pltpu.make_async_copy(tok_hbm.at[:, cols], tokq.at[n], tok_sem.at[n])
        q_copies[n].start()
    tok_copies = {}
    for n, j in enumerate((2, 0)):
        cols = pl.ds(pl.multiple_of(where_to[j] * rows, LANE), rows)
        tok_copies[n] = pltpu.make_async_copy(tok_hbm.at[:, cols], tokv.at[n], tok_sem.at[2 + n])
        tok_copies[n].start()
    w_copies = []
    for k in range(chunks):
        part = pl.ds(k * piece, piece)
        for p in range(2):
            w_copies.append(
                pltpu.make_async_copy(w_hbm.at[part, p, :], wv.at[p, part], w_sem.at[p, k])
            )
            w_copies[-1].start()
    in_copies[1].start()

    barrier = pltpu.get_barrier_semaphore()
    greeted = [{"row": where_to[j]} for j in (1, 2, 3)] + [{"col": c} for c in (col_x, col_z, col_far)]
    for device in greeted:
        pl.semaphore_signal(barrier, inc=1, device_id=device, device_id_type=pl.DeviceIdType.MESH)

    before = lax.broadcasted_iota(jnp.int32, (LANE, LANE), 0)
    after = lax.broadcasted_iota(jnp.int32, (LANE, LANE), 1)
    ladder = jnp.where(before < after, 1.0, 0.0).astype(jnp.bfloat16)
    every = jnp.ones((LANE, LANE), jnp.bfloat16)
    in_copies[0].wait()
    named = jnp.logical_or(routes[0:1, :] == 0, routes[1:2, :] == 0)
    flag = jnp.where(named, 1.0, 0.0)
    mask = jnp.broadcast_to(flag, (16, toks)).astype(jnp.bfloat16)
    earlier = jnp.zeros((16, LANE), jnp.float32)
    places = []
    for k in range(toks // LANE):
        part = mask[:, k * LANE : (k + 1) * LANE]
        places.append(earlier + jnp.dot(part, ladder, preferred_element_type=jnp.float32))
        earlier = earlier + jnp.dot(part, every, preferred_element_type=jnp.float32)
    place = jnp.concatenate(places, axis=1)[0:1, :].astype(jnp.int32)
    slot_id = lax.broadcasted_iota(jnp.int32, (slots, toks), 0)
    pick = jnp.where(slot_id == place, flag, 0.0).astype(jnp.bfloat16)
    pl.semaphore_wait(barrier, len(greeted))

    def routed(c, q):
        j = (1, 3)[c // 2]
        return sc.at[
            pl.ds(j * slots + (c % 2) * half, half),
            pl.ds(pl.multiple_of(q * quarter, LANE), quarter),
        ]

    y_copies = []
    for c in range(4):
        n = c // 2
        if c % 2 == 0:
            q_copies[n].wait()
            qsend[n] = jnp.dot(pick, tokq[n], preferred_element_type=jnp.float32).astype(jnp.bfloat16)
        y_copies.append(
            moved(
                qsend.at[n, pl.ds((c % 2) * half, half)],
                routed(c, quarter_of),
                y_send.at[c],
                y_recv.at[c],
                {"row": where_to[(1, 3)[n]]},
            )
        )
        y_copies[-1].start()
    tok_copies[0].wait()
    psendt[...] = jnp.dot(pick, tokv[0], preferred_element_type=jnp.float32).astype(jnp.bfloat16)
    t_copy = moved(psendt, sc.at[pl.ds(2 * slots, slots)], pt_send.at[0], pt_recv.at[0], {"row": partner})
    t_copy.start()
    tok_copies[1].wait()
    sc[0:slots, :] = jnp.dot(pick, tokv[1], preferred_element_type=jnp.float32).astype(jnp.bfloat16)

    x_copies = [moved(routed(c, quarter_of), routed(c, quarter_of), x_send.at[c], x_recv.at[c], {"col": col_x}) for c in range(4)]
    z_copies = [moved(routed(c, quarter_of), routed(c, quarter_of), z_send.at[c], z_recv.at[c], {"col": col_z}) for c in range(4)]
    for n in range(2):
        x_copies.append(
            moved(routed(2 * n + 1, quarter_z), routed(2 * n + 1, quarter_z), x_send.at[4 + n], x_recv.at[4 + n], {"col": col_x})
        )
        z_copies.append(
            moved(routed(2 * n, quarter_x), routed(2 * n, quarter_x), z_send.at[4 + n], z_recv.at[4 + n], {"col": col_z})
        )

    def pass_on(c):
        y_copies[c].wait_recv()
        x_copies[c].start()
        z_copies[c].start()

    def pass_x(n):
        x_copies[2 * n].wait_recv()
        z_copies[4 + n].start()

    def pass_z(n):
        z_copies[2 * n + 1].wait_recv()
        x_copies[4 + n].start()

    folded[...] = jnp.zeros(folded.shape, jnp.float32)

    def fold_chunk(k):
        for p in range(2):
            w_copies[2 * k + p].wait()

        def fold(t, carry):
            cols = pl.ds(pl.multiple_of(t * LANE, LANE), LANE)
            for p in range(2):
                tile = jnp.abs(wv[p, k * piece : (k + 1) * piece, cols])
                best = jnp.max(tile.reshape(-1, SUB, LANE), axis=0)
                folded[p, :, cols] = jnp.maximum(folded[p, :, cols], best)
            return carry

        lax.fori_loop(0, tiles, fold, 0)

    order = (
        lambda: pass_on(0), lambda: pass_on(1), lambda: pass_on(2),
        lambda: pass_x(0), lambda: pass_z(0), lambda: pass_on(3),
    )
    for k in range(chunks):
        fold_chunk(k)
        if k < len(order):
            order[k]()
    for p in range(2):
        cmx[0, p : p + 1, :] = jnp.max(folded[p], axis=0, keepdims=True)
    c_copies = []
    for j in (1, 2, 3):
        c_copies.append(
            moved(cmx.at[0], cmx.at[j], c_send.at[j - 1], c_recv.at[j - 1], {"row": where_to[j]})
        )
        c_copies[-1].start()
    turned[:, 0:slots] = sc[0:slots, :].T
    t_copy.wait()
    turned[:, 2 * slots : 3 * slots] = sc[2 * slots : 3 * slots, :].T
    pass_x(1)
    pass_z(1)
    for copy in c_copies:
        copy.wait()
    cm_ref[...] = jnp.maximum(jnp.maximum(cmx[0], cmx[1]), jnp.maximum(cmx[2], cmx[3]))
    tops[...] = jnp.zeros(tops.shape, jnp.float32)
    in_copies[1].wait()
    for c in range(4):
        y_copies[c].wait_send()
    for copies, late in ((x_copies, (1, 3, 4, 5)), (z_copies, (0, 2, 4, 5))):
        for c in late:
            copies[c].wait_recv()

    def scale_row(t, p):
        cols = pl.ds(pl.multiple_of(t * LANE, LANE), LANE)
        return (cm_ref[p : p + 1, cols] + epsilon) / quant_range

    def swap(t):
        return moved(psend.at[t], prec.at[t], p_send.at[t], p_recv.at[t], {"row": partner})

    def cross(t):
        return moved(xsend.at[t], xrec.at[t], xs_send.at[t], xs_recv.at[t], {"row": across})

    def grad_block(t, j):
        return ga.at[t, pl.ds(j * slots, slots)]

    def share_across(t):
        return moved(grad_block(t, 0), grad_block(t, 1), ga_send.at[t], ga_recv.at[t], {"row": across})

    def share_partner(t):
        return moved(grad_block(t, 0), grad_block(t, 2), gp_send.at[t], gp_recv.at[t], {"row": partner})

    def forward(t):
        return moved(grad_block(t, 1), grad_block(t, 3), gf_send.at[t], gf_recv.at[t], {"row": partner})

    depth = 3 * BLK

    def step(i, carry):
        @pl.when(i < tiles)
        def _():
            t = i
            halves = []
            for p in range(2):
                w = wv[p, :, pl.ds(pl.multiple_of(t * LANE, LANE), LANE)]
                halves.append((w * (1.0 / scale_row(t, p))).astype(jnp.bfloat16))
            quantized = jnp.concatenate(halves, axis=1)
            term = jnp.dot(sc[...], quantized, preferred_element_type=jnp.float32)
            slot = lax.rem(t, 2)
            psend[t] = term[2 * slots :].astype(jnp.bfloat16)
            keep[slot] = term[: 2 * slots]
            swap(t).start()

        @pl.when(jnp.logical_and(i >= 1, i < tiles + 1))
        def _():
            t = i - 1
            slot = lax.rem(t, 2)
            swap(t).wait_recv()
            own[t] = keep[slot, :slots] + prec[t, :slots].astype(jnp.float32)
            xsend[t] = (keep[slot, slots:] + prec[t, slots:].astype(jnp.float32)).astype(jnp.bfloat16)
            cross(t).start()

        @pl.when(i == 1)
        def _():
            for j in (1, 3):
                turned[:, j * slots : (j + 1) * slots] = sc[j * slots : (j + 1) * slots, :].T

        @pl.when(jnp.logical_and(i >= 1 + LEAD, i < tiles + 1 + LEAD))
        def _():
            t = i - 1 - LEAD
            cross(t).wait_recv()
            total = own[t] + xrec[t].astype(jnp.float32)
            gate_pre = total[:, :LANE] * scale_row(t, 0)
            up_pre = total[:, LANE:] * scale_row(t, 1)
            gate_sig = jax.nn.sigmoid(gate_pre)
            gate_act = gate_pre * gate_sig
            cols = pl.ds(pl.multiple_of(t * LANE, LANE), LANE)
            hid[:, cols] = (gate_act * up_pre).astype(jnp.bfloat16)
            upstream = dh[:, cols].astype(jnp.float32)
            grad_gate = upstream * up_pre * gate_sig * (1.0 + gate_pre * (1.0 - gate_sig))
            grad_up = upstream * gate_act
            ga[t, 0:slots, :] = jnp.concatenate([grad_gate, grad_up], axis=1).astype(jnp.bfloat16)
            share_across(t).start()
            share_partner(t).start()

        @pl.when(jnp.logical_and(i >= 3 + LEAD, i < tiles + 3 + LEAD))
        def _():
            t = i - 3 - LEAD
            share_across(t).wait_recv()
            forward(t).start()

        @pl.when(i >= 4 + LEAD)
        def _():
            t = i - 4 - LEAD
            share_partner(t).wait_recv()
            forward(t).wait_recv()
            cols = pl.ds(pl.multiple_of(t * 2 * LANE, 2 * LANE), 2 * LANE)
            for k in range(rows // depth):
                grad = jnp.dot(turned[k * depth : (k + 1) * depth, :], ga[t], preferred_element_type=jnp.float32)
                grad_ref[k * depth : (k + 1) * depth, cols] = grad.astype(jnp.bfloat16)
                for b in range(3):
                    for p in range(2):
                        n = 2 * (3 * k + b) + p
                        tile = jnp.abs(grad[b * BLK : (b + 1) * BLK, p * LANE : (p + 1) * LANE])
                        tops[n] = jnp.maximum(tops[n], jnp.max(tile.reshape(-1, SUB, LANE), axis=0))

        return carry

    lax.fori_loop(0, tiles + 4 + LEAD, step, 0)

    for n in range(tops.shape[0]):
        bmx[0, n : n + 1, :] = jnp.max(tops[n], axis=0, keepdims=True)
    b_copies = []
    for k in range(1, group):
        b_copies.append(
            moved(bmx.at[0], bmx.at[k], b_send.at[k - 1], b_recv.at[k - 1], {"col": lax.rem(col + k, group)})
        )
        b_copies[-1].start()

    def finish(t, carry):
        swap(t).wait_send()
        cross(t).wait_send()
        share_across(t).wait_send()
        share_partner(t).wait_send()
        forward(t).wait_send()
        return carry

    lax.fori_loop(0, tiles, finish, 0)
    for copies in (x_copies, z_copies):
        for copy in copies:
            copy.wait_send()
    for copy in b_copies:
        copy.wait()
    best = bmx[0]
    for k in range(1, group):
        best = jnp.maximum(best, bmx[k])
    block_max = jnp.max(best, axis=1, keepdims=True)
    inv_ref[...] = jnp.broadcast_to(1.0 / (block_max + epsilon), inv_ref.shape)


def update_kernel(inv_ref, cm_ref, grad_ref, hid, wv, out_hbm, update_hbm, new_hbm, uv, nv, u_sem, n_sem, h_sem):
    blocks = u_sem.shape[1]
    columns = wv.shape[2]
    tiles = columns // LANE

    def part(b):
        return pl.ds(pl.multiple_of(b * BLK, BLK), BLK)

    def put_update(b, p):
        return pltpu.make_async_copy(uv.at[p, part(b)], update_hbm.at[part(b), p, :], u_sem.at[p, b])

    def put_new(b, p):
        return pltpu.make_async_copy(nv.at[p, part(b)], new_hbm.at[part(b), p, :], n_sem.at[p, b])

    def step(b, carry):
        for p in range(2):
            inverse = inv_ref[pl.ds(2 * b + p, 1), :]
            for t in range(tiles):
                cols = slice(t * LANE, (t + 1) * LANE)
                at = (2 * t + p) * LANE
                update = grad_ref[part(b), at : at + LANE].astype(jnp.float32) * inverse
                uv[p, part(b), cols] = update
                nv[p, part(b), cols] = wv[p, part(b), cols] - (learn_rate * cm_ref[p : p + 1, cols]) * update
            put_update(b, p).start()
            put_new(b, p).start()
        return carry

    def finish(b, carry):
        for p in range(2):
            put_update(b, p).wait()
            put_new(b, p).wait()
        return carry

    put_hidden = pltpu.make_async_copy(hid, out_hbm, h_sem.at[0])
    put_hidden.start()
    lax.fori_loop(0, blocks, step, 0)
    lax.fori_loop(0, blocks, finish, 0)
    put_hidden.wait()


def on_device(tokens, routes, w_master, d_hidden):
    rows, _, columns = w_master.shape
    slots = d_hidden.shape[0]
    toks = tokens.shape[0]
    aligned = columns % LANE == 0 and rows % (12 * BLK) == 0 and slots % 32 == 0 and toks % LANE == 0
    if lax.axis_size("row") != 4 or lax.axis_size("col") != 8 or not aligned:
        return on_device_plain(tokens, routes, w_master, d_hidden)
    group = lax.axis_size("col")
    tiles = columns // LANE
    bf16, f32 = jnp.bfloat16, jnp.float32
    chunks = 6
    blocks = rows // BLK
    vmem = pl.BlockSpec(memory_space=pltpu.VMEM)
    hbm = pl.BlockSpec(memory_space=pltpu.HBM)
    dma = pltpu.SemaphoreType.DMA
    wide = 2 * LANE
    hidden, grad, colmax, inverse, master = pl.pallas_call(
        layer_kernel,
        name="layer_exchange",
        out_shape=(
            jax.ShapeDtypeStruct((slots, columns), bf16),
            pltpu.VMEM((rows, 2 * columns), bf16),
            jax.ShapeDtypeStruct((2, columns), f32),
            jax.ShapeDtypeStruct((2 * blocks, LANE), f32),
            pltpu.VMEM((2, rows, columns), f32),
        ),
        in_specs=[hbm, hbm, hbm, hbm],
        out_specs=(vmem,) * 5,
        scratch_shapes=[
            pltpu.VMEM((2, toks), jnp.int32),
            pltpu.VMEM((slots, columns), bf16),
            pltpu.VMEM((2, toks, rows), bf16),
            pltpu.VMEM((2, toks, rows // 4), bf16),
            pltpu.VMEM((slots, rows), bf16),
            pltpu.VMEM((2, slots, rows // 4), bf16),
            pltpu.VMEM((4 * slots, rows), bf16),
            pltpu.VMEM((rows, 4 * slots), bf16),
            pltpu.VMEM((2, SUB, columns), f32),
            pltpu.VMEM((4, 2, columns), f32),
            pltpu.VMEM((tiles, 2 * slots, wide), bf16),
            pltpu.VMEM((tiles, 2 * slots, wide), bf16),
            pltpu.VMEM((2, 2 * slots, wide), f32),
            pltpu.VMEM((tiles, slots, wide), f32),
            pltpu.VMEM((tiles, slots, wide), bf16),
            pltpu.VMEM((tiles, slots, wide), bf16),
            pltpu.VMEM((tiles, 4 * slots, wide), bf16),
            pltpu.VMEM((2 * blocks, SUB, LANE), f32),
            pltpu.VMEM((group, 2 * blocks, LANE), f32),
            dma((2,)),
            dma((4,)),
            dma((2, chunks)),
            dma((1,)),
            dma((1,)),
            dma((4,)),
            dma((4,)),
            dma((6,)),
            dma((6,)),
            dma((6,)),
            dma((6,)),
            dma((3,)),
            dma((3,)),
            dma((group - 1,)),
            dma((group - 1,)),
        ]
        + [dma((tiles,))] * 10,
        compiler_params=pltpu.CompilerParams(
            collective_id=0, has_side_effects=True, vmem_limit_bytes=26 * 1024 * 1024
        ),
    )(*(pltpu.with_memory_space_constraint(x, pltpu.HBM) for x in (routes.T, d_hidden, tokens, w_master)))
    hidden, update, new_master = pl.pallas_call(
        update_kernel,
        name="master_update",
        out_shape=(jax.ShapeDtypeStruct((slots, columns), bf16),)
        + (jax.ShapeDtypeStruct(w_master.shape, f32),) * 2,
        in_specs=[vmem] * 5,
        out_specs=(hbm, hbm, hbm),
        scratch_shapes=[
            pltpu.VMEM((2, rows, columns), f32),
            pltpu.VMEM((2, rows, columns), f32),
            dma((2, blocks)),
            dma((2, blocks)),
            dma((1,)),
        ],
        compiler_params=pltpu.CompilerParams(vmem_limit_bytes=30 * 1024 * 1024),
    )(inverse, colmax, grad, hidden, master)
    return (hidden, update, new_master)


def solution(mesh):
    in_specs = (P("row", None), P("row", None), P("row", None, "col"), P("row", "col"))
    out_specs = (P("row", "col"), P("row", None, "col"), P("row", None, "col"))
    return jax.shard_map(
        on_device, mesh=mesh, in_specs=in_specs, out_specs=out_specs, check_vma=False
    )
```

time: 144 us -> 83.1 us (0.58)
  Pallas kernels: 112 us -> 82.3 us
  blocking collectives: 21.6 us -> 0 us
  local copies, waits for them, and re-layouts: 8.81 us -> 0 us
    pmax x1 -> x0, blocking collectives: 21.6 us -> none  [on_device(): block_max = lax.pmax(jnp.max(tops, axis=(2, 3)).reshape(-1), 'col')]
    pallas_call x2 -> x1, Pallas kernels: 93 us -> 72.4 us  [on_device(): pl.pallas_call(layer_kernel, name='layer_exchange', out_shape=(jax.ShapeD...]
    pallas_call x1, Pallas kernels: 18.6 us -> 9.85 us  [on_device(): pl.pallas_call(update_kernel, name='master_update', out_shape=(jax.ShapeD...]
    unnamed x11 -> x0, local copies, waits for them, and re-layouts: 8.11 us -> none
where the time goes in v1:
time: 83.1 us; the launch traced here: 82.9 us
  Pallas kernels  82.3 us (99%)
    pallas_call x1, Pallas kernels, on_device(): pl.pallas_call(layer_kernel, name='layer_exchange', out_shape=(jax.ShapeD...  72.4 us
    pallas_call x1, Pallas kernels, on_device(): pl.pallas_call(update_kernel, name='master_update', out_shape=(jax.ShapeD...  9.85 us

profile of v1, /device:TPU:0, one launch (start us, length us, event | category | flops | bytes accessed | tf_op | source)
XLA Modules:
  0.0 82.9 jit_solution(18398821394700452243)
XLA Ops:
  0.6 72.4 %layer_exchange.1 = (bf16[192,1152]{1,0:T(8,128)(2,1)S(1)}, bf16[1536,2304]{1,0:T(8,128)(2,1)S(1)}, f32[2,1152]{1,0:T(2,128)S(1)}, f32[24,128]{1,0:T(8,128)S(1)}, f32[2,1536,1152]{2,1,0:T(8,128)S(1)}) custom-call(s32[2,768]{1,0:T(2,128)} %bitcast.1, bf16[192,1152]{1,0:T(8,128)(2,1)} %dh_hbm.1, bf16[768,6144]{1,0:T(8,128)(2,1)} %tok_hbm.1, f32[1536,2,1152]{2,1,0:T(2,128)} %w_hbm.1), custom_call_target="tpu_custom_call" | custom-call | tf_op jit(solution)/shard_map/layer_exchange/pallas_call | solution.py:449
  73.1 9.9 %master_update.1 = (bf16[192,1152]{1,0:T(8,128)(2,1)}, f32[1536,2,1152]{2,1,0:T(2,128)}, f32[1536,2,1152]{2,1,0:T(2,128)}) custom-call(f32[24,128]{1,0:T(8,128)S(1)} %get-tuple-element.8.inv_ref, f32[2,1152]{1,0:T(2,128)S(1)} %get-tuple-element.9.cm_ref, bf16[1536,2304]{1,0:T(8,128)(2,1)S(1)} %get-tuple-element.10.grad_ref, ...), custom_call_target="tpu_custom_call" | custom-call | tf_op jit(solution)/shard_map/master_update/pallas_call | solution.py:502

commit v2 on v1

--- a/solution.py
+++ b/solution.py
@@ -65,7 +65,7 @@
 
 LANE = 128
 SUB = 8
-LEAD = 3
+LEAD = 6
 
 
 def moved(src, dst, send, recv, to):
@@ -85,11 +85,11 @@
 
 def layer_kernel(
     routes_hbm, dh_hbm, tok_hbm, w_hbm, hid, grad_ref, cm_ref, inv_ref, wv,
-    routes, dh, tokv, tokq, psendt, qsend, sc, turned, folded, cmx,
-    psend, prec, keep, own, xsend, xrec, ga, tops, bmx,
+    routes, dh, tokv, tokq, psendt, qsend, sc, turned, folded, cmx, wq,
+    esend, erec, own, lsend, lrec, keep, xsend, xrec, ga, tops, bmx,
     in_sem, tok_sem, w_sem, pt_send, pt_recv, y_send, y_recv, x_send, x_recv, z_send, z_recv,
-    c_send, c_recv, b_send, b_recv,
-    p_send, p_recv, xs_send, xs_recv, ga_send, ga_recv, gp_send, gp_recv, gf_send, gf_recv,
+    c_send, c_recv, b_send, b_recv, l_send, l_recv, xs_send, xs_recv,
+    e_send, e_recv, ga_send, ga_recv, gp_send, gp_recv, gf_send, gf_recv,
 ):
     me = lax.axis_index("row")
     col = lax.axis_index("col")
@@ -97,14 +97,11 @@
     partner = me + 1 - 2 * core
     across = lax.rem(me + 2, 4)
     diag = lax.rem(partner + 2, 4)
-    where_to = (me, across, partner, diag)
     group = bmx.shape[0]
     col_x = flipped(col, 1)
     col_z = flipped(col, 2)
     col_far = flipped(col, 4)
     quarter_of = lax.rem(col, 4)
-    quarter_x = lax.rem(col_x, 4)
-    quarter_z = lax.rem(col_z, 4)
     tiles = ga.shape[0]
     slots = hid.shape[0]
     rows = sc.shape[1]
@@ -119,16 +116,17 @@
         pltpu.make_async_copy(dh_hbm, dh, in_sem.at[1]),
     )
     in_copies[0].start()
-    q_copies = {}
-    for n, j in enumerate((1, 3)):
-        cols = pl.ds(pl.multiple_of(where_to[j] * rows + quarter_of * quarter, LANE), quarter)
-        q_copies[n] = pltpu.make_async_copy(tok_hbm.at[:, cols], tokq.at[n], tok_sem.at[n])
-        q_copies[n].start()
-    tok_copies = {}
-    for n, j in enumerate((2, 0)):
-        cols = pl.ds(pl.multiple_of(where_to[j] * rows, LANE), rows)
-        tok_copies[n] = pltpu.make_async_copy(tok_hbm.at[:, cols], tokv.at[n], tok_sem.at[2 + n])
-        tok_copies[n].start()
+    q_copies = []
+    for n in range(4):
+        q = (quarter_of, 3 - quarter_of)[n // 2]
+        cols = pl.ds(pl.multiple_of((across, diag)[n % 2] * rows + q * quarter, LANE), quarter)
+        q_copies.append(pltpu.make_async_copy(tok_hbm.at[:, cols], tokq.at[n], tok_sem.at[n]))
+        q_copies[-1].start()
+    tok_copies = []
+    for n in range(2):
+        cols = pl.ds(pl.multiple_of((partner, me)[n] * rows, LANE), rows)
+        tok_copies.append(pltpu.make_async_copy(tok_hbm.at[:, cols], tokv.at[n], tok_sem.at[4 + n]))
+        tok_copies[-1].start()
     w_copies = []
     for k in range(chunks):
         part = pl.ds(k * piece, piece)
@@ -140,7 +138,7 @@
     in_copies[1].start()
 
     barrier = pltpu.get_barrier_semaphore()
-    greeted = [{"row": where_to[j]} for j in (1, 2, 3)] + [{"col": c} for c in (col_x, col_z, col_far)]
+    greeted = [{"row": r} for r in (across, diag, partner)] + [{"col": c} for c in (col_x, col_z, col_far)]
     for device in greeted:
         pl.semaphore_signal(barrier, inc=1, device_id=device, device_id_type=pl.DeviceIdType.MESH)
 
@@ -163,58 +161,52 @@
     pick = jnp.where(slot_id == place, flag, 0.0).astype(jnp.bfloat16)
     pl.semaphore_wait(barrier, len(greeted))
 
-    def routed(c, q):
-        j = (1, 3)[c // 2]
+    def routed(h, jj, q):
         return sc.at[
-            pl.ds(j * slots + (c % 2) * half, half),
+            pl.ds((2 + h) * slots + jj * half, half),
             pl.ds(pl.multiple_of(q * quarter, LANE), quarter),
         ]
 
-    y_copies = []
-    for c in range(4):
-        n = c // 2
-        if c % 2 == 0:
-            q_copies[n].wait()
-            qsend[n] = jnp.dot(pick, tokq[n], preferred_element_type=jnp.float32).astype(jnp.bfloat16)
-        y_copies.append(
-            moved(
-                qsend.at[n, pl.ds((c % 2) * half, half)],
-                routed(c, quarter_of),
-                y_send.at[c],
-                y_recv.at[c],
-                {"row": where_to[(1, 3)[n]]},
-            )
+    def y_copy(h, n):
+        return moved(
+            qsend.at[n, pl.ds(h * half, half)],
+            routed(h, n % 2, (quarter_of, 3 - quarter_of)[n // 2]),
+            y_send.at[4 * h + n],
+            y_recv.at[4 * h + n],
+            {"row": (across, diag)[n % 2]},
         )
-        y_copies[-1].start()
+
+    for n in range(4):
+        q_copies[n].wait()
+        qsend[n] = jnp.dot(pick, tokq[n], preferred_element_type=jnp.float32).astype(jnp.bfloat16)
+        y_copy(0, n).start()
+    for n in range(4):
+        y_copy(1, n).start()
     tok_copies[0].wait()
     psendt[...] = jnp.dot(pick, tokv[0], preferred_element_type=jnp.float32).astype(jnp.bfloat16)
-    t_copy = moved(psendt, sc.at[pl.ds(2 * slots, slots)], pt_send.at[0], pt_recv.at[0], {"row": partner})
+    t_copy = moved(psendt, sc.at[pl.ds(slots, slots)], pt_send.at[0], pt_recv.at[0], {"row": partner})
     t_copy.start()
     tok_copies[1].wait()
     sc[0:slots, :] = jnp.dot(pick, tokv[1], preferred_element_type=jnp.float32).astype(jnp.bfloat16)
 
-    x_copies = [moved(routed(c, quarter_of), routed(c, quarter_of), x_send.at[c], x_recv.at[c], {"col": col_x}) for c in range(4)]
-    z_copies = [moved(routed(c, quarter_of), routed(c, quarter_of), z_send.at[c], z_recv.at[c], {"col": col_z}) for c in range(4)]
-    for n in range(2):
-        x_copies.append(
-            moved(routed(2 * n + 1, quarter_z), routed(2 * n + 1, quarter_z), x_send.at[4 + n], x_recv.at[4 + n], {"col": col_x})
+    def side_copies(h, jj):
+        here = routed(h, jj, quarter_of)
+        n = 2 * h + jj
+        return (
+            moved(here, here, x_send.at[n], x_recv.at[n], {"col": col_x}),
+            moved(here, here, z_send.at[n], z_recv.at[n], {"col": col_z}),
         )
-        z_copies.append(
-            moved(routed(2 * n, quarter_x), routed(2 * n, quarter_x), z_send.at[4 + n], z_recv.at[4 + n], {"col": col_z})
-        )
-
-    def pass_on(c):
-        y_copies[c].wait_recv()
-        x_copies[c].start()
-        z_copies[c].start()
-
-    def pass_x(n):
-        x_copies[2 * n].wait_recv()
-        z_copies[4 + n].start()
-
-    def pass_z(n):
-        z_copies[2 * n + 1].wait_recv()
-        x_copies[4 + n].start()
+
+    def pass_on(h, jj):
+        y_copy(h, jj).wait_recv()
+        for copy in side_copies(h, jj):
+            copy.start()
+
+    def arrived(h):
+        for jj in range(2):
+            y_copy(h, 2 + jj).wait_recv()
+            for copy in side_copies(h, jj):
+                copy.wait_recv()
 
     folded[...] = jnp.zeros(folded.shape, jnp.float32)
 
@@ -232,96 +224,114 @@
 
         lax.fori_loop(0, tiles, fold, 0)
 
-    order = (
-        lambda: pass_on(0), lambda: pass_on(1), lambda: pass_on(2),
-        lambda: pass_x(0), lambda: pass_z(0), lambda: pass_on(3),
-    )
     for k in range(chunks):
         fold_chunk(k)
-        if k < len(order):
-            order[k]()
+        if k == 2:
+            pass_on(0, 0)
+        if k == 4:
+            pass_on(0, 1)
     for p in range(2):
         cmx[0, p : p + 1, :] = jnp.max(folded[p], axis=0, keepdims=True)
     c_copies = []
-    for j in (1, 2, 3):
-        c_copies.append(
-            moved(cmx.at[0], cmx.at[j], c_send.at[j - 1], c_recv.at[j - 1], {"row": where_to[j]})
-        )
+    for j, row in enumerate((partner, across, diag)):
+        c_copies.append(moved(cmx.at[0], cmx.at[j + 1], c_send.at[j], c_recv.at[j], {"row": row}))
         c_copies[-1].start()
     turned[:, 0:slots] = sc[0:slots, :].T
     t_copy.wait()
-    turned[:, 2 * slots : 3 * slots] = sc[2 * slots : 3 * slots, :].T
-    pass_x(1)
-    pass_z(1)
+    turned[:, slots : 2 * slots] = sc[slots : 2 * slots, :].T
+    tops[...] = jnp.zeros(tops.shape, jnp.float32)
+    in_copies[1].wait()
     for copy in c_copies:
         copy.wait()
     cm_ref[...] = jnp.maximum(jnp.maximum(cmx[0], cmx[1]), jnp.maximum(cmx[2], cmx[3]))
-    tops[...] = jnp.zeros(tops.shape, jnp.float32)
-    in_copies[1].wait()
-    for c in range(4):
-        y_copies[c].wait_send()
-    for copies, late in ((x_copies, (1, 3, 4, 5)), (z_copies, (0, 2, 4, 5))):
-        for c in late:
-            copies[c].wait_recv()
+    arrived(0)
 
     def scale_row(t, p):
         cols = pl.ds(pl.multiple_of(t * LANE, LANE), LANE)
         return (cm_ref[p : p + 1, cols] + epsilon) / quant_range
 
-    def swap(t):
-        return moved(psend.at[t], prec.at[t], p_send.at[t], p_recv.at[t], {"row": partner})
-
-    def cross(t):
-        return moved(xsend.at[t], xrec.at[t], xs_send.at[t], xs_recv.at[t], {"row": across})
+    def swap_late(n):
+        return moved(lsend.at[n], lrec.at[n], l_send.at[n], l_recv.at[n], {"row": partner})
+
+    def swap_early(t):
+        return moved(esend.at[t], erec.at[t], e_send.at[t], e_recv.at[t], {"row": partner})
+
+    def cross(n):
+        return moved(xsend.at[n], xrec.at[n], xs_send.at[n], xs_recv.at[n], {"row": across})
 
     def grad_block(t, j):
         return ga.at[t, pl.ds(j * slots, slots)]
 
     def share_across(t):
-        return moved(grad_block(t, 0), grad_block(t, 1), ga_send.at[t], ga_recv.at[t], {"row": across})
+        return moved(grad_block(t, 0), grad_block(t, 2), ga_send.at[t], ga_recv.at[t], {"row": across})
 
     def share_partner(t):
-        return moved(grad_block(t, 0), grad_block(t, 2), gp_send.at[t], gp_recv.at[t], {"row": partner})
+        return moved(grad_block(t, 0), grad_block(t, 1), gp_send.at[t], gp_recv.at[t], {"row": partner})
 
     def forward(t):
-        return moved(grad_block(t, 1), grad_block(t, 3), gf_send.at[t], gf_recv.at[t], {"row": partner})
+        return moved(grad_block(t, 2), grad_block(t, 3), gf_send.at[t], gf_recv.at[t], {"row": partner})
 
     depth = 3 * BLK
+    finals = tiles + LEAD
 
     def step(i, carry):
+        @pl.when(i == 1)
+        def _():
+            pass_on(1, 0)
+
+        @pl.when(i == 2)
+        def _():
+            pass_on(1, 1)
+
+        @pl.when(i == tiles)
+        def _():
+            arrived(1)
+
         @pl.when(i < tiles)
         def _():
-            t = i
-            halves = []
             for p in range(2):
-                w = wv[p, :, pl.ds(pl.multiple_of(t * LANE, LANE), LANE)]
-                halves.append((w * (1.0 / scale_row(t, p))).astype(jnp.bfloat16))
-            quantized = jnp.concatenate(halves, axis=1)
-            term = jnp.dot(sc[...], quantized, preferred_element_type=jnp.float32)
-            slot = lax.rem(t, 2)
-            psend[t] = term[2 * slots :].astype(jnp.bfloat16)
-            keep[slot] = term[: 2 * slots]
-            swap(t).start()
-
-        @pl.when(jnp.logical_and(i >= 1, i < tiles + 1))
-        def _():
-            t = i - 1
-            slot = lax.rem(t, 2)
-            swap(t).wait_recv()
-            own[t] = keep[slot, :slots] + prec[t, :slots].astype(jnp.float32)
-            xsend[t] = (keep[slot, slots:] + prec[t, slots:].astype(jnp.float32)).astype(jnp.bfloat16)
-            cross(t).start()
-
-        @pl.when(i == 1)
-        def _():
-            for j in (1, 3):
-                turned[:, j * slots : (j + 1) * slots] = sc[j * slots : (j + 1) * slots, :].T
-
-        @pl.when(jnp.logical_and(i >= 1 + LEAD, i < tiles + 1 + LEAD))
-        def _():
-            t = i - 1 - LEAD
+                w = wv[p, :, pl.ds(pl.multiple_of(i * LANE, LANE), LANE)]
+                wq[i, :, p * LANE : (p + 1) * LANE] = (w * (1.0 / scale_row(i, p))).astype(jnp.bfloat16)
+
+        @pl.when(i < 2 * tiles)
+        def _():
+            h = i // tiles
+            t = lax.rem(i, tiles)
+            late = sc[pl.ds(pl.multiple_of((2 + h) * slots, 16), slots), :]
+            term = jnp.dot(late, wq[t], preferred_element_type=jnp.float32)
+            lsend[i] = term[half:].astype(jnp.bfloat16)
+            keep[lax.rem(i, 2)] = term[:half]
+            swap_late(i).start()
+
+        @pl.when(jnp.logical_and(i >= 1, i < 2 * tiles + 1))
+        def _():
+            n = i - 1
+            swap_late(n).wait_recv()
+            xsend[n] = (keep[lax.rem(n, 2)] + lrec[n].astype(jnp.float32)).astype(jnp.bfloat16)
+            cross(n).start()
+
+        @pl.when(jnp.logical_and(i >= tiles, i < 2 * tiles))
+        def _():
+            t = i - tiles
+            term = jnp.dot(sc[0 : 2 * slots, :], wq[t], preferred_element_type=jnp.float32)
+            esend[t] = term[slots:].astype(jnp.bfloat16)
+            own[t] = term[:slots]
+            swap_early(t).start()
+
+        @pl.when(i == tiles + 1)
+        def _():
+            for jj in range(2):
+                block = [sc[(2 + h) * slots + jj * half : (2 + h) * slots + (jj + 1) * half, :] for h in range(2)]
+                turned[:, (2 + jj) * slots : (3 + jj) * slots] = jnp.concatenate(block, axis=0).T
+
+        @pl.when(jnp.logical_and(i >= finals, i < finals + tiles))
+        def _():
+            t = i - finals
+            swap_early(t).wait_recv()
             cross(t).wait_recv()
-            total = own[t] + xrec[t].astype(jnp.float32)
+            cross(tiles + t).wait_recv()
+            others = jnp.concatenate([xrec[t], xrec[tiles + t]], axis=0).astype(jnp.float32)
+            total = own[t] + erec[t].astype(jnp.float32) + others
             gate_pre = total[:, :LANE] * scale_row(t, 0)
             up_pre = total[:, LANE:] * scale_row(t, 1)
             gate_sig = jax.nn.sigmoid(gate_pre)
@@ -335,15 +345,15 @@
             share_across(t).start()
             share_partner(t).start()
 
-        @pl.when(jnp.logical_and(i >= 3 + LEAD, i < tiles + 3 + LEAD))
-        def _():
-            t = i - 3 - LEAD
+        @pl.when(jnp.logical_and(i >= finals + 2, i < finals + 2 + tiles))
+        def _():
+            t = i - finals - 2
             share_across(t).wait_recv()
             forward(t).start()
 
-        @pl.when(i >= 4 + LEAD)
-        def _():
-            t = i - 4 - LEAD
+        @pl.when(i >= finals + 3)
+        def _():
+            t = i - finals - 3
             share_partner(t).wait_recv()
             forward(t).wait_recv()
             cols = pl.ds(pl.multiple_of(t * 2 * LANE, 2 * LANE), 2 * LANE)
@@ -358,7 +368,7 @@
 
         return carry
 
-    lax.fori_loop(0, tiles + 4 + LEAD, step, 0)
+    lax.fori_loop(0, finals + 3 + tiles, step, 0)
 
     for n in range(tops.shape[0]):
         bmx[0, n : n + 1, :] = jnp.max(tops[n], axis=0, keepdims=True)
@@ -370,17 +380,22 @@
         b_copies[-1].start()
 
     def finish(t, carry):
-        swap(t).wait_send()
-        cross(t).wait_send()
+        for n in (t, tiles + t):
+            swap_late(n).wait_send()
+            cross(n).wait_send()
+        swap_early(t).wait_send()
         share_across(t).wait_send()
         share_partner(t).wait_send()
         forward(t).wait_send()
         return carry
 
     lax.fori_loop(0, tiles, finish, 0)
-    for copies in (x_copies, z_copies):
-        for copy in copies:
-            copy.wait_send()
+    for h in range(2):
+        for n in range(4):
+            y_copy(h, n).wait_send()
+        for jj in range(2):
+            for copy in side_copies(h, jj):
+                copy.wait_send()
     for copy in b_copies:
         copy.wait()
     best = bmx[0]
@@ -450,10 +465,10 @@
         layer_kernel,
         name="layer_exchange",
         out_shape=(
-            jax.ShapeDtypeStruct((slots, columns), bf16),
+            pltpu.VMEM((slots, columns), bf16),
             pltpu.VMEM((rows, 2 * columns), bf16),
-            jax.ShapeDtypeStruct((2, columns), f32),
-            jax.ShapeDtypeStruct((2 * blocks, LANE), f32),
+            pltpu.VMEM((2, columns), f32),
+            pltpu.VMEM((2 * blocks, LANE), f32),
             pltpu.VMEM((2, rows, columns), f32),
         ),
         in_specs=[hbm, hbm, hbm, hbm],
@@ -462,41 +477,40 @@
             pltpu.VMEM((2, toks), jnp.int32),
             pltpu.VMEM((slots, columns), bf16),
             pltpu.VMEM((2, toks, rows), bf16),
-            pltpu.VMEM((2, toks, rows // 4), bf16),
+            pltpu.VMEM((4, toks, rows // 4), bf16),
             pltpu.VMEM((slots, rows), bf16),
-            pltpu.VMEM((2, slots, rows // 4), bf16),
+            pltpu.VMEM((4, slots, rows // 4), bf16),
             pltpu.VMEM((4 * slots, rows), bf16),
             pltpu.VMEM((rows, 4 * slots), bf16),
             pltpu.VMEM((2, SUB, columns), f32),
             pltpu.VMEM((4, 2, columns), f32),
-            pltpu.VMEM((tiles, 2 * slots, wide), bf16),
-            pltpu.VMEM((tiles, 2 * slots, wide), bf16),
-            pltpu.VMEM((2, 2 * slots, wide), f32),
-            pltpu.VMEM((tiles, slots, wide), f32),
+            pltpu.VMEM((tiles, rows, wide), bf16),
             pltpu.VMEM((tiles, slots, wide), bf16),
             pltpu.VMEM((tiles, slots, wide), bf16),
+            pltpu.VMEM((tiles, slots, wide), f32),
+            pltpu.VMEM((2 * tiles, slots // 2, wide), bf16),
+            pltpu.VMEM((2 * tiles, slots // 2, wide), bf16),
+            pltpu.VMEM((2, slots // 2, wide), f32),
+            pltpu.VMEM((2 * tiles, slots // 2, wide), bf16),
+            pltpu.VMEM((2 * tiles, slots // 2, wide), bf16),
             pltpu.VMEM((tiles, 4 * slots, wide), bf16),
             pltpu.VMEM((2 * blocks, SUB, LANE), f32),
             pltpu.VMEM((group, 2 * blocks, LANE), f32),
             dma((2,)),
-            dma((4,)),
+            dma((6,)),
             dma((2, chunks)),
             dma((1,)),
             dma((1,)),
-            dma((4,)),
-            dma((4,)),
-            dma((6,)),
-            dma((6,)),
-            dma((6,)),
-            dma((6,)),
-            dma((3,)),
-            dma((3,)),
-            dma((group - 1,)),
-            dma((group - 1,)),
+            dma((8,)),
+            dma((8,)),
         ]
-        + [dma((tiles,))] * 10,
+        + [dma((4,))] * 4
+        + [dma((3,))] * 2
+        + [dma((group - 1,))] * 2
+        + [dma((2 * tiles,))] * 4
+        + [dma((tiles,))] * 8,
         compiler_params=pltpu.CompilerParams(
-            collective_id=0, has_side_effects=True, vmem_limit_bytes=26 * 1024 * 1024
+            collective_id=0, has_side_effects=True, vmem_limit_bytes=34 * 1024 * 1024
         ),
     )(*(pltpu.with_memory_space_constraint(x, pltpu.HBM) for x in (routes.T, d_hidden, tokens, w_master)))
     hidden, update, new_master = pl.pallas_call(

time: 83.1 us -> 81.2 us (0.977)
  Pallas kernels: 82.3 us -> 80.4 us
    pallas_call x1, Pallas kernels: 72.4 us -> 70.5 us  [on_device(): pl.pallas_call(layer_kernel, name='layer_exchange', out_shape=(pltpu.VMEM...]
where the time goes in v2:
time: 81.2 us; the launch traced here: 81 us
  Pallas kernels  80.4 us (99%)
    pallas_call x1, Pallas kernels, on_device(): pl.pallas_call(layer_kernel, name='layer_exchange', out_shape=(pltpu.VMEM...  70.5 us
    pallas_call x1, Pallas kernels, on_device(): pl.pallas_call(update_kernel, name='master_update', out_shape=(jax.ShapeD...  9.85 us

profile of v2, /device:TPU:0, one launch (start us, length us, event | category | flops | bytes accessed | tf_op | source)
XLA Modules:
  0.0 81.0 jit_solution(15450365374710049398)
XLA Ops:
  0.6 70.5 %layer_exchange.1 = (bf16[192,1152]{1,0:T(8,128)(2,1)S(1)}, bf16[1536,2304]{1,0:T(8,128)(2,1)S(1)}, f32[2,1152]{1,0:T(2,128)S(1)}, f32[24,128]{1,0:T(8,128)S(1)}, f32[2,1536,1152]{2,1,0:T(8,128)S(1)}) custom-call(s32[2,768]{1,0:T(2,128)} %bitcast.1, bf16[192,1152]{1,0:T(8,128)(2,1)} %dh_hbm.1, bf16[768,6144]{1,0:T(8,128)(2,1)} %tok_hbm.1, f32[1536,2,1152]{2,1,0:T(2,128)} %w_hbm.1), custom_call_target="tpu_custom_call" | custom-call | tf_op jit(solution)/shard_map/layer_exchange/pallas_call | solution.py:464
  71.2 9.9 %master_update.1 = (bf16[192,1152]{1,0:T(8,128)(2,1)}, f32[1536,2,1152]{2,1,0:T(2,128)}, f32[1536,2,1152]{2,1,0:T(2,128)}) custom-call(f32[24,128]{1,0:T(8,128)S(1)} %get-tuple-element.8.inv_ref, f32[2,1152]{1,0:T(2,128)S(1)} %get-tuple-element.9.cm_ref, bf16[1536,2304]{1,0:T(8,128)(2,1)S(1)} %get-tuple-element.10.grad_ref, ...), custom_call_target="tpu_custom_call" | custom-call | tf_op jit(solution)/shard_map/master_update/pallas_call | solution.py:516

commit v3 on v2

--- a/solution.py
+++ b/solution.py
@@ -65,7 +65,9 @@
 
 LANE = 128
 SUB = 8
-LEAD = 6
+LEAD = 9
+SWAP = 3
+SHARE = 3
 
 
 def moved(src, dst, send, recv, to):
@@ -122,11 +124,6 @@
         cols = pl.ds(pl.multiple_of((across, diag)[n % 2] * rows + q * quarter, LANE), quarter)
         q_copies.append(pltpu.make_async_copy(tok_hbm.at[:, cols], tokq.at[n], tok_sem.at[n]))
         q_copies[-1].start()
-    tok_copies = []
-    for n in range(2):
-        cols = pl.ds(pl.multiple_of((partner, me)[n] * rows, LANE), rows)
-        tok_copies.append(pltpu.make_async_copy(tok_hbm.at[:, cols], tokv.at[n], tok_sem.at[4 + n]))
-        tok_copies[-1].start()
     w_copies = []
     for k in range(chunks):
         part = pl.ds(k * piece, piece)
@@ -135,6 +132,11 @@
                 pltpu.make_async_copy(w_hbm.at[part, p, :], wv.at[p, part], w_sem.at[p, k])
             )
             w_copies[-1].start()
+    tok_copies = []
+    for n in range(2):
+        cols = pl.ds(pl.multiple_of((partner, me)[n] * rows, LANE), rows)
+        tok_copies.append(pltpu.make_async_copy(tok_hbm.at[:, cols], tokv.at[n], tok_sem.at[4 + n]))
+        tok_copies[-1].start()
     in_copies[1].start()
 
     barrier = pltpu.get_barrier_semaphore()
@@ -180,15 +182,6 @@
         q_copies[n].wait()
         qsend[n] = jnp.dot(pick, tokq[n], preferred_element_type=jnp.float32).astype(jnp.bfloat16)
         y_copy(0, n).start()
-    for n in range(4):
-        y_copy(1, n).start()
-    tok_copies[0].wait()
-    psendt[...] = jnp.dot(pick, tokv[0], preferred_element_type=jnp.float32).astype(jnp.bfloat16)
-    t_copy = moved(psendt, sc.at[pl.ds(slots, slots)], pt_send.at[0], pt_recv.at[0], {"row": partner})
-    t_copy.start()
-    tok_copies[1].wait()
-    sc[0:slots, :] = jnp.dot(pick, tokv[1], preferred_element_type=jnp.float32).astype(jnp.bfloat16)
-
     def side_copies(h, jj):
         here = routed(h, jj, quarter_of)
         n = 2 * h + jj
@@ -226,16 +219,22 @@
 
     for k in range(chunks):
         fold_chunk(k)
-        if k == 2:
-            pass_on(0, 0)
-        if k == 4:
-            pass_on(0, 1)
     for p in range(2):
         cmx[0, p : p + 1, :] = jnp.max(folded[p], axis=0, keepdims=True)
     c_copies = []
-    for j, row in enumerate((partner, across, diag)):
+    for j, row in enumerate((across, diag, partner)):
         c_copies.append(moved(cmx.at[0], cmx.at[j + 1], c_send.at[j], c_recv.at[j], {"row": row}))
         c_copies[-1].start()
+    for n in range(4):
+        y_copy(1, n).start()
+    pass_on(0, 0)
+    tok_copies[0].wait()
+    psendt[...] = jnp.dot(pick, tokv[0], preferred_element_type=jnp.float32).astype(jnp.bfloat16)
+    t_copy = moved(psendt, sc.at[pl.ds(slots, slots)], pt_send.at[0], pt_recv.at[0], {"row": partner})
+    t_copy.start()
+    pass_on(0, 1)
+    tok_copies[1].wait()
+    sc[0:slots, :] = jnp.dot(pick, tokv[1], preferred_element_type=jnp.float32).astype(jnp.bfloat16)
     turned[:, 0:slots] = sc[0:slots, :].T
     t_copy.wait()
     turned[:, slots : 2 * slots] = sc[slots : 2 * slots, :].T
@@ -300,14 +299,14 @@
             late = sc[pl.ds(pl.multiple_of((2 + h) * slots, 16), slots), :]
             term = jnp.dot(late, wq[t], preferred_element_type=jnp.float32)
             lsend[i] = term[half:].astype(jnp.bfloat16)
-            keep[lax.rem(i, 2)] = term[:half]
+            keep[lax.rem(i, SWAP + 1)] = term[:half]
             swap_late(i).start()
 
-        @pl.when(jnp.logical_and(i >= 1, i < 2 * tiles + 1))
-        def _():
-            n = i - 1
+        @pl.when(jnp.logical_and(i >= SWAP, i < 2 * tiles + SWAP))
+        def _():
+            n = i - SWAP
             swap_late(n).wait_recv()
-            xsend[n] = (keep[lax.rem(n, 2)] + lrec[n].astype(jnp.float32)).astype(jnp.bfloat16)
+            xsend[n] = (keep[lax.rem(n, SWAP + 1)] + lrec[n].astype(jnp.float32)).astype(jnp.bfloat16)
             cross(n).start()
 
         @pl.when(jnp.logical_and(i >= tiles, i < 2 * tiles))
@@ -345,15 +344,15 @@
             share_across(t).start()
             share_partner(t).start()
 
-        @pl.when(jnp.logical_and(i >= finals + 2, i < finals + 2 + tiles))
-        def _():
-            t = i - finals - 2
+        @pl.when(jnp.logical_and(i >= finals + SHARE, i < finals + SHARE + tiles))
+        def _():
+            t = i - finals - SHARE
             share_across(t).wait_recv()
             forward(t).start()
 
-        @pl.when(i >= finals + 3)
-        def _():
-            t = i - finals - 3
+        @pl.when(i >= finals + SHARE + 1)
+        def _():
+            t = i - finals - SHARE - 1
             share_partner(t).wait_recv()
             forward(t).wait_recv()
             cols = pl.ds(pl.multiple_of(t * 2 * LANE, 2 * LANE), 2 * LANE)
@@ -368,7 +367,7 @@
 
         return carry
 
-    lax.fori_loop(0, finals + 3 + tiles, step, 0)
+    lax.fori_loop(0, finals + SHARE + 1 + tiles, step, 0)
 
     for n in range(tops.shape[0]):
         bmx[0, n : n + 1, :] = jnp.max(tops[n], axis=0, keepdims=True)
@@ -490,7 +489,7 @@
             pltpu.VMEM((tiles, slots, wide), f32),
             pltpu.VMEM((2 * tiles, slots // 2, wide), bf16),
             pltpu.VMEM((2 * tiles, slots // 2, wide), bf16),
-            pltpu.VMEM((2, slots // 2, wide), f32),
+            pltpu.VMEM((SWAP + 1, slots // 2, wide), f32),
             pltpu.VMEM((2 * tiles, slots // 2, wide), bf16),
             pltpu.VMEM((2 * tiles, slots // 2, wide), bf16),
             pltpu.VMEM((tiles, 4 * slots, wide), bf16),

time: 81.2 us -> 77.1 us (0.950)
  Pallas kernels: 80.4 us -> 76.3 us
    pallas_call x1, Pallas kernels: 70.5 us -> 66.4 us  [on_device(): pl.pallas_call(layer_kernel, name='layer_exchange', out_shape=(pltpu.VMEM...]
where the time goes in v3:
time: 77.1 us; the launch traced here: 76.9 us
  Pallas kernels  76.3 us (99%)
    pallas_call x1, Pallas kernels, on_device(): pl.pallas_call(layer_kernel, name='layer_exchange', out_shape=(pltpu.VMEM...  66.4 us
    pallas_call x1, Pallas kernels, on_device(): pl.pallas_call(update_kernel, name='master_update', out_shape=(jax.ShapeD...  9.85 us

profile of v3, /device:TPU:0, one launch (start us, length us, event | category | flops | bytes accessed | tf_op | source)
XLA Modules:
  0.0 76.9 jit_solution(4985426474787902251)
XLA Ops:
  0.6 66.4 %layer_exchange.1 = (bf16[192,1152]{1,0:T(8,128)(2,1)S(1)}, bf16[1536,2304]{1,0:T(8,128)(2,1)S(1)}, f32[2,1152]{1,0:T(2,128)S(1)}, f32[24,128]{1,0:T(8,128)S(1)}, f32[2,1536,1152]{2,1,0:T(8,128)S(1)}) custom-call(s32[2,768]{1,0:T(2,128)} %bitcast.1, bf16[192,1152]{1,0:T(8,128)(2,1)} %dh_hbm.1, bf16[768,6144]{1,0:T(8,128)(2,1)} %tok_hbm.1, f32[1536,2,1152]{2,1,0:T(2,128)} %w_hbm.1), custom_call_target="tpu_custom_call" | custom-call | tf_op jit(solution)/shard_map/layer_exchange/pallas_call | solution.py:463
  67.1 9.9 %master_update.1 = (bf16[192,1152]{1,0:T(8,128)(2,1)}, f32[1536,2,1152]{2,1,0:T(2,128)}, f32[1536,2,1152]{2,1,0:T(2,128)}) custom-call(f32[24,128]{1,0:T(8,128)S(1)} %get-tuple-element.8.inv_ref, f32[2,1152]{1,0:T(2,128)S(1)} %get-tuple-element.9.cm_ref, bf16[1536,2304]{1,0:T(8,128)(2,1)S(1)} %get-tuple-element.10.grad_ref, ...), custom_call_target="tpu_custom_call" | custom-call | tf_op jit(solution)/shard_map/master_update/pallas_call | solution.py:515

commit v4 on v2

--- a/solution.py
+++ b/solution.py
@@ -65,7 +65,10 @@
 
 LANE = 128
 SUB = 8
-LEAD = 6
+CUT = (1, 2)
+FIRST = 3
+SWAP = 1
+SHARE = 4
 
 
 def moved(src, dst, send, recv, to):
@@ -79,6 +82,10 @@
     )
 
 
+def wide_part(slots):
+    return slots - slots * CUT[0] // CUT[1] // 16 * 16
+
+
 def flipped(index, bit):
     return index + bit - 2 * bit * lax.rem(index // bit, 2)
 
@@ -86,10 +93,10 @@
 def layer_kernel(
     routes_hbm, dh_hbm, tok_hbm, w_hbm, hid, grad_ref, cm_ref, inv_ref, wv,
     routes, dh, tokv, tokq, psendt, qsend, sc, turned, folded, cmx, wq,
-    esend, erec, own, lsend, lrec, keep, xsend, xrec, ga, tops, bmx,
+    esend, erec, own, lsend, lrec, keep, xsend, xrec, ga, tops, flat, bmx,
     in_sem, tok_sem, w_sem, pt_send, pt_recv, y_send, y_recv, x_send, x_recv, z_send, z_recv,
     c_send, c_recv, b_send, b_recv, l_send, l_recv, xs_send, xs_recv,
-    e_send, e_recv, ga_send, ga_recv, gp_send, gp_recv, gf_send, gf_recv,
+    ga_send, ga_recv, gp_send, gp_recv, gf_send, gf_recv, e_send, e_recv,
 ):
     me = lax.axis_index("row")
     col = lax.axis_index("col")
@@ -109,7 +116,9 @@
     chunks = w_sem.shape[1]
     piece = rows // chunks
     quarter = rows // 4
-    half = slots // 2
+    sizes = (slots - wide_part(slots), wide_part(slots))
+    starts = (0, sizes[0])
+    bases = (2 * slots, 2 * slots + 2 * sizes[0])
 
     in_copies = (
         pltpu.make_async_copy(routes_hbm, routes, in_sem.at[0]),
@@ -163,13 +172,13 @@
 
     def routed(h, jj, q):
         return sc.at[
-            pl.ds((2 + h) * slots + jj * half, half),
+            pl.ds(bases[h] + jj * sizes[h], sizes[h]),
             pl.ds(pl.multiple_of(q * quarter, LANE), quarter),
         ]
 
     def y_copy(h, n):
         return moved(
-            qsend.at[n, pl.ds(h * half, half)],
+            qsend.at[n, pl.ds(starts[h], sizes[h])],
             routed(h, n % 2, (quarter_of, 3 - quarter_of)[n // 2]),
             y_send.at[4 * h + n],
             y_recv.at[4 * h + n],
@@ -178,17 +187,9 @@
 
     for n in range(4):
         q_copies[n].wait()
-        qsend[n] = jnp.dot(pick, tokq[n], preferred_element_type=jnp.float32).astype(jnp.bfloat16)
+        many = slots if n < 2 else sizes[0]
+        qsend[n, 0:many] = jnp.dot(pick[0:many], tokq[n], preferred_element_type=jnp.float32).astype(jnp.bfloat16)
         y_copy(0, n).start()
-    for n in range(4):
-        y_copy(1, n).start()
-    tok_copies[0].wait()
-    psendt[...] = jnp.dot(pick, tokv[0], preferred_element_type=jnp.float32).astype(jnp.bfloat16)
-    t_copy = moved(psendt, sc.at[pl.ds(slots, slots)], pt_send.at[0], pt_recv.at[0], {"row": partner})
-    t_copy.start()
-    tok_copies[1].wait()
-    sc[0:slots, :] = jnp.dot(pick, tokv[1], preferred_element_type=jnp.float32).astype(jnp.bfloat16)
-
     def side_copies(h, jj):
         here = routed(h, jj, quarter_of)
         n = 2 * h + jj
@@ -202,11 +203,25 @@
         for copy in side_copies(h, jj):
             copy.start()
 
-    def arrived(h):
+    def relay_x():
+        block = routed(1, 1, lax.rem(col_z, 4))
+        return moved(block, block, x_send.at[4], x_recv.at[4], {"col": col_x})
+
+    def relay_z():
+        block = routed(1, 0, lax.rem(col_x, 4))
+        return moved(block, block, z_send.at[4], z_recv.at[4], {"col": col_z})
+
+    def arrived_first():
         for jj in range(2):
-            y_copy(h, 2 + jj).wait_recv()
-            for copy in side_copies(h, jj):
+            y_copy(0, 2 + jj).wait_recv()
+            for copy in side_copies(0, jj):
                 copy.wait_recv()
+
+    def arrived_second():
+        side_copies(1, 1)[0].wait_recv()
+        side_copies(1, 0)[1].wait_recv()
+        relay_z().wait_recv()
+        relay_x().wait_recv()
 
     folded[...] = jnp.zeros(folded.shape, jnp.float32)
 
@@ -224,19 +239,27 @@
 
         lax.fori_loop(0, tiles, fold, 0)
 
-    for k in range(chunks):
+    tok_copies[0].wait()
+    psendt[...] = jnp.dot(pick, tokv[0], preferred_element_type=jnp.float32).astype(jnp.bfloat16)
+    t_copy = moved(psendt, sc.at[pl.ds(slots, slots)], pt_send.at[0], pt_recv.at[0], {"row": partner})
+    t_copy.start()
+    tok_copies[1].wait()
+    sc[0:slots, :] = jnp.dot(pick, tokv[1], preferred_element_type=jnp.float32).astype(jnp.bfloat16)
+    pass_on(0, 0)
+    fold_chunk(0)
+    fold_chunk(1)
+    turned[:, 0:slots] = sc[0:slots, :].T
+    pass_on(0, 1)
+    for k in range(2, chunks):
         fold_chunk(k)
-        if k == 2:
-            pass_on(0, 0)
-        if k == 4:
-            pass_on(0, 1)
     for p in range(2):
         cmx[0, p : p + 1, :] = jnp.max(folded[p], axis=0, keepdims=True)
     c_copies = []
-    for j, row in enumerate((partner, across, diag)):
+    for j, row in enumerate((across, diag, partner)):
         c_copies.append(moved(cmx.at[0], cmx.at[j + 1], c_send.at[j], c_recv.at[j], {"row": row}))
         c_copies[-1].start()
-    turned[:, 0:slots] = sc[0:slots, :].T
+    for n in range(2):
+        y_copy(1, n).start()
     t_copy.wait()
     turned[:, slots : 2 * slots] = sc[slots : 2 * slots, :].T
     tops[...] = jnp.zeros(tops.shape, jnp.float32)
@@ -244,118 +267,160 @@
     for copy in c_copies:
         copy.wait()
     cm_ref[...] = jnp.maximum(jnp.maximum(cmx[0], cmx[1]), jnp.maximum(cmx[2], cmx[3]))
-    arrived(0)
+    arrived_first()
 
     def scale_row(t, p):
         cols = pl.ds(pl.multiple_of(t * LANE, LANE), LANE)
         return (cm_ref[p : p + 1, cols] + epsilon) / quant_range
 
-    def swap_late(n):
-        return moved(lsend.at[n], lrec.at[n], l_send.at[n], l_recv.at[n], {"row": partner})
+    def swap_late(h, t):
+        n, some = h * tiles + t, pl.ds(0, sizes[h])
+        return moved(lsend.at[n, some], lrec.at[n, some], l_send.at[n], l_recv.at[n], {"row": partner})
 
     def swap_early(t):
         return moved(esend.at[t], erec.at[t], e_send.at[t], e_recv.at[t], {"row": partner})
 
-    def cross(n):
-        return moved(xsend.at[n], xrec.at[n], xs_send.at[n], xs_recv.at[n], {"row": across})
-
-    def grad_block(t, j):
-        return ga.at[t, pl.ds(j * slots, slots)]
-
-    def share_across(t):
-        return moved(grad_block(t, 0), grad_block(t, 2), ga_send.at[t], ga_recv.at[t], {"row": across})
-
-    def share_partner(t):
-        return moved(grad_block(t, 0), grad_block(t, 1), gp_send.at[t], gp_recv.at[t], {"row": partner})
-
-    def forward(t):
-        return moved(grad_block(t, 2), grad_block(t, 3), gf_send.at[t], gf_recv.at[t], {"row": partner})
+    def cross(h, t):
+        n, some = h * tiles + t, pl.ds(0, sizes[h])
+        return moved(xsend.at[n, some], xrec.at[n, some], xs_send.at[n], xs_recv.at[n], {"row": across})
+
+    def grad_block(h, t, j):
+        return ga.at[t, pl.ds(j * slots + starts[h], sizes[h])]
+
+    def share_across(h, t):
+        n = h * tiles + t
+        return moved(grad_block(h, t, 0), grad_block(h, t, 2), ga_send.at[n], ga_recv.at[n], {"row": across})
+
+    def share_partner(h, t):
+        n = h * tiles + t
+        return moved(grad_block(h, t, 0), grad_block(h, t, 1), gp_send.at[n], gp_recv.at[n], {"row": partner})
+
+    def forward(h, t):
+        n = h * tiles + t
+        return moved(grad_block(h, t, 2), grad_block(h, t, 3), gf_send.at[n], gf_recv.at[n], {"row": partner})
+
+    def offer(h, t, term):
+        n, size = h * tiles + t, sizes[h]
+        lsend[n, 0:size] = term[size:].astype(jnp.bfloat16)
+        swap_late(h, t).start()
+        keep[lax.rem(n, SWAP + 1), 0:size] = term[:size]
+
+    def cross_late(h, t):
+        n, size = h * tiles + t, sizes[h]
+        swap_late(h, t).wait_recv()
+        both = keep[lax.rem(n, SWAP + 1), 0:size] + lrec[n, 0:size].astype(jnp.float32)
+        xsend[n, 0:size] = both.astype(jnp.bfloat16)
+        cross(h, t).start()
+
+    def finalize(h, t):
+        mine = slice(starts[h], starts[h] + sizes[h])
+        cross(h, t).wait_recv()
+        others = xrec[h * tiles + t, 0 : sizes[h]].astype(jnp.float32)
+        total = own[t, mine] + erec[t, mine].astype(jnp.float32) + others
+        gate_pre = total[:, :LANE] * scale_row(t, 0)
+        up_pre = total[:, LANE:] * scale_row(t, 1)
+        gate_sig = jax.nn.sigmoid(gate_pre)
+        gate_act = gate_pre * gate_sig
+        cols = pl.ds(pl.multiple_of(t * LANE, LANE), LANE)
+        hid[mine, cols] = (gate_act * up_pre).astype(jnp.bfloat16)
+        upstream = dh[mine, cols].astype(jnp.float32)
+        grad_gate = upstream * up_pre * gate_sig * (1.0 + gate_pre * (1.0 - gate_sig))
+        grad_up = upstream * gate_act
+        ga[t, mine, :] = jnp.concatenate([grad_gate, grad_up], axis=1).astype(jnp.bfloat16)
+        share_across(h, t).start()
+        share_partner(h, t).start()
+
+    def hand_over(h, t):
+        share_across(h, t).wait_recv()
+        forward(h, t).start()
 
     depth = 3 * BLK
-    finals = tiles + LEAD
+    first_final = SWAP + FIRST
+    second = tiles + 1
+    second_final = second + tiles + SWAP
+    second_share = second_final + SHARE
+    last = second_share + 1 + tiles
+
+    def during(i, start):
+        return jnp.logical_and(i >= start, i < start + tiles)
 
     def step(i, carry):
-        @pl.when(i == 1)
+        @pl.when(i == 2)
         def _():
             pass_on(1, 0)
 
-        @pl.when(i == 2)
+        @pl.when(i == 3)
         def _():
             pass_on(1, 1)
 
-        @pl.when(i == tiles)
-        def _():
-            arrived(1)
+        @pl.when(i == 5)
+        def _():
+            side_copies(1, 0)[0].wait_recv()
+            relay_z().start()
+
+        @pl.when(i == 7)
+        def _():
+            side_copies(1, 1)[1].wait_recv()
+            relay_x().start()
 
         @pl.when(i < tiles)
         def _():
             for p in range(2):
                 w = wv[p, :, pl.ds(pl.multiple_of(i * LANE, LANE), LANE)]
                 wq[i, :, p * LANE : (p + 1) * LANE] = (w * (1.0 / scale_row(i, p))).astype(jnp.bfloat16)
-
-        @pl.when(i < 2 * tiles)
-        def _():
-            h = i // tiles
-            t = lax.rem(i, tiles)
-            late = sc[pl.ds(pl.multiple_of((2 + h) * slots, 16), slots), :]
-            term = jnp.dot(late, wq[t], preferred_element_type=jnp.float32)
-            lsend[i] = term[half:].astype(jnp.bfloat16)
-            keep[lax.rem(i, 2)] = term[:half]
-            swap_late(i).start()
-
-        @pl.when(jnp.logical_and(i >= 1, i < 2 * tiles + 1))
-        def _():
-            n = i - 1
-            swap_late(n).wait_recv()
-            xsend[n] = (keep[lax.rem(n, 2)] + lrec[n].astype(jnp.float32)).astype(jnp.bfloat16)
-            cross(n).start()
-
-        @pl.when(jnp.logical_and(i >= tiles, i < 2 * tiles))
-        def _():
-            t = i - tiles
-            term = jnp.dot(sc[0 : 2 * slots, :], wq[t], preferred_element_type=jnp.float32)
-            esend[t] = term[slots:].astype(jnp.bfloat16)
-            own[t] = term[:slots]
-            swap_early(t).start()
-
-        @pl.when(i == tiles + 1)
+            term = jnp.dot(sc[0 : bases[1], :], wq[i], preferred_element_type=jnp.float32)
+            offer(0, i, term[2 * slots :])
+            esend[i] = term[slots : 2 * slots].astype(jnp.bfloat16)
+            swap_early(i).start()
+            own[i] = term[:slots]
+
+        @pl.when(during(i, SWAP))
+        def _():
+            cross_late(0, i - SWAP)
+
+        @pl.when(during(i, first_final))
+        def _():
+            t = i - first_final
+            swap_early(t).wait_recv()
+            finalize(0, t)
+
+        @pl.when(i == second)
+        def _():
+            arrived_second()
+
+        @pl.when(during(i, second))
+        def _():
+            t = i - second
+            offer(1, t, jnp.dot(sc[bases[1] :, :], wq[t], preferred_element_type=jnp.float32))
+
+        @pl.when(during(i, second + SWAP))
+        def _():
+            cross_late(1, i - second - SWAP)
+
+        @pl.when(i == second + 1)
         def _():
             for jj in range(2):
-                block = [sc[(2 + h) * slots + jj * half : (2 + h) * slots + (jj + 1) * half, :] for h in range(2)]
+                block = [sc[bases[h] + jj * sizes[h] : bases[h] + (jj + 1) * sizes[h], :] for h in range(2)]
                 turned[:, (2 + jj) * slots : (3 + jj) * slots] = jnp.concatenate(block, axis=0).T
 
-        @pl.when(jnp.logical_and(i >= finals, i < finals + tiles))
-        def _():
-            t = i - finals
-            swap_early(t).wait_recv()
-            cross(t).wait_recv()
-            cross(tiles + t).wait_recv()
-            others = jnp.concatenate([xrec[t], xrec[tiles + t]], axis=0).astype(jnp.float32)
-            total = own[t] + erec[t].astype(jnp.float32) + others
-            gate_pre = total[:, :LANE] * scale_row(t, 0)
-            up_pre = total[:, LANE:] * scale_row(t, 1)
-            gate_sig = jax.nn.sigmoid(gate_pre)
-            gate_act = gate_pre * gate_sig
-            cols = pl.ds(pl.multiple_of(t * LANE, LANE), LANE)
-            hid[:, cols] = (gate_act * up_pre).astype(jnp.bfloat16)
-            upstream = dh[:, cols].astype(jnp.float32)
-            grad_gate = upstream * up_pre * gate_sig * (1.0 + gate_pre * (1.0 - gate_sig))
-            grad_up = upstream * gate_act
-            ga[t, 0:slots, :] = jnp.concatenate([grad_gate, grad_up], axis=1).astype(jnp.bfloat16)
-            share_across(t).start()
-            share_partner(t).start()
-
-        @pl.when(jnp.logical_and(i >= finals + 2, i < finals + 2 + tiles))
-        def _():
-            t = i - finals - 2
-            share_across(t).wait_recv()
-            forward(t).start()
-
-        @pl.when(i >= finals + 3)
-        def _():
-            t = i - finals - 3
-            share_partner(t).wait_recv()
-            forward(t).wait_recv()
+        @pl.when(during(i, second + SWAP))
+        def _():
+            hand_over(0, i - second - SWAP)
+
+        @pl.when(during(i, second_final))
+        def _():
+            finalize(1, i - second_final)
+
+        @pl.when(during(i, second_share))
+        def _():
+            hand_over(1, i - second_share)
+
+        @pl.when(i >= second_share + 1)
+        def _():
+            t = i - second_share - 1
+            for h in range(2):
+                share_partner(h, t).wait_recv()
+                forward(h, t).wait_recv()
             cols = pl.ds(pl.multiple_of(t * 2 * LANE, 2 * LANE), 2 * LANE)
             for k in range(rows // depth):
                 grad = jnp.dot(turned[k * depth : (k + 1) * depth, :], ga[t], preferred_element_type=jnp.float32)
@@ -368,10 +433,17 @@
 
         return carry
 
-    lax.fori_loop(0, finals + 3 + tiles, step, 0)
+    lax.fori_loop(0, last, step, 0)
 
     for n in range(tops.shape[0]):
-        bmx[0, n : n + 1, :] = jnp.max(tops[n], axis=0, keepdims=True)
+        flat[n : n + 1, :] = jnp.max(tops[n], axis=0, keepdims=True)
+    lane = lax.broadcasted_iota(jnp.int32, (SUB, LANE), 1)
+    packs = tops.shape[0] // SUB
+    packed = jnp.zeros((SUB, LANE), jnp.float32)
+    for k in range(packs):
+        widest = jnp.max(flat[k * SUB : (k + 1) * SUB, :], axis=1, keepdims=True)
+        packed = jnp.where(lane == k, widest, packed)
+    bmx[0] = packed
     b_copies = []
     for k in range(1, group):
         b_copies.append(
@@ -380,18 +452,17 @@
         b_copies[-1].start()
 
     def finish(t, carry):
-        for n in (t, tiles + t):
-            swap_late(n).wait_send()
-            cross(n).wait_send()
         swap_early(t).wait_send()
-        share_across(t).wait_send()
-        share_partner(t).wait_send()
-        forward(t).wait_send()
+        for h in range(2):
+            for copy in (swap_late, cross, share_across, share_partner, forward):
+                copy(h, t).wait_send()
         return carry
 
     lax.fori_loop(0, tiles, finish, 0)
+    relay_x().wait_send()
+    relay_z().wait_send()
     for h in range(2):
-        for n in range(4):
+        for n in range(4 - 2 * h):
             y_copy(h, n).wait_send()
         for jj in range(2):
             for copy in side_copies(h, jj):
@@ -401,8 +472,9 @@
     best = bmx[0]
     for k in range(1, group):
         best = jnp.maximum(best, bmx[k])
-    block_max = jnp.max(best, axis=1, keepdims=True)
-    inv_ref[...] = jnp.broadcast_to(1.0 / (block_max + epsilon), inv_ref.shape)
+    for k in range(packs):
+        block_max = jnp.max(jnp.where(lane == k, best, 0.0), axis=1, keepdims=True)
+        inv_ref[k * SUB : (k + 1) * SUB, :] = jnp.broadcast_to(1.0 / (block_max + epsilon), (SUB, LANE))
 
 
 def update_kernel(inv_ref, cm_ref, grad_ref, hid, wv, out_hbm, update_hbm, new_hbm, uv, nv, u_sem, n_sem, h_sem):
@@ -450,6 +522,7 @@
     slots = d_hidden.shape[0]
     toks = tokens.shape[0]
     aligned = columns % LANE == 0 and rows % (12 * BLK) == 0 and slots % 32 == 0 and toks % LANE == 0
+    aligned = aligned and 2 * rows // BLK <= SUB * LANE
     if lax.axis_size("row") != 4 or lax.axis_size("col") != 8 or not aligned:
         return on_device_plain(tokens, routes, w_master, d_hidden)
     group = lax.axis_size("col")
@@ -488,27 +561,28 @@
             pltpu.VMEM((tiles, slots, wide), bf16),
             pltpu.VMEM((tiles, slots, wide), bf16),
             pltpu.VMEM((tiles, slots, wide), f32),
-            pltpu.VMEM((2 * tiles, slots // 2, wide), bf16),
-            pltpu.VMEM((2 * tiles, slots // 2, wide), bf16),
-            pltpu.VMEM((2, slots // 2, wide), f32),
-            pltpu.VMEM((2 * tiles, slots // 2, wide), bf16),
-            pltpu.VMEM((2 * tiles, slots // 2, wide), bf16),
+            pltpu.VMEM((2 * tiles, wide_part(slots), wide), bf16),
+            pltpu.VMEM((2 * tiles, wide_part(slots), wide), bf16),
+            pltpu.VMEM((SWAP + 1, wide_part(slots), wide), f32),
+            pltpu.VMEM((2 * tiles, wide_part(slots), wide), bf16),
+            pltpu.VMEM((2 * tiles, wide_part(slots), wide), bf16),
             pltpu.VMEM((tiles, 4 * slots, wide), bf16),
             pltpu.VMEM((2 * blocks, SUB, LANE), f32),
-            pltpu.VMEM((group, 2 * blocks, LANE), f32),
+            pltpu.VMEM((2 * blocks, LANE), f32),
+            pltpu.VMEM((group, SUB, LANE), f32),
             dma((2,)),
             dma((6,)),
             dma((2, chunks)),
             dma((1,)),
             dma((1,)),
-            dma((8,)),
-            dma((8,)),
+            dma((6,)),
+            dma((6,)),
         ]
-        + [dma((4,))] * 4
+        + [dma((5,))] * 4
         + [dma((3,))] * 2
         + [dma((group - 1,))] * 2
-        + [dma((2 * tiles,))] * 4
-        + [dma((tiles,))] * 8,
+        + [dma((2 * tiles,))] * 10
+        + [dma((tiles,))] * 2,
         compiler_params=pltpu.CompilerParams(
             collective_id=0, has_side_effects=True, vmem_limit_bytes=34 * 1024 * 1024
         ),

time: 81.2 us -> 76.5 us (0.942)
  Pallas kernels: 80.4 us -> 75.7 us
    pallas_call x1, Pallas kernels: 70.5 us -> 65.8 us  [on_device(): pl.pallas_call(layer_kernel, name='layer_exchange', out_shape=(pltpu.VMEM...]
where the time goes in v4:
time: 76.5 us; the launch traced here: 76.3 us
  Pallas kernels  75.7 us (99%)
    pallas_call x1, Pallas kernels, on_device(): pl.pallas_call(layer_kernel, name='layer_exchange', out_shape=(pltpu.VMEM...  65.8 us
    pallas_call x1, Pallas kernels, on_device(): pl.pallas_call(update_kernel, name='master_update', out_shape=(jax.ShapeD...  9.85 us

profile of v4, /device:TPU:0, one launch (start us, length us, event | category | flops | bytes accessed | tf_op | source)
XLA Modules:
  0.0 76.3 jit_solution(11066567883393959888)
XLA Ops:
  0.6 65.8 %layer_exchange.1 = (bf16[192,1152]{1,0:T(8,128)(2,1)S(1)}, bf16[1536,2304]{1,0:T(8,128)(2,1)S(1)}, f32[2,1152]{1,0:T(2,128)S(1)}, f32[24,128]{1,0:T(8,128)S(1)}, f32[2,1536,1152]{2,1,0:T(8,128)S(1)}) custom-call(s32[2,768]{1,0:T(2,128)} %bitcast.1, bf16[192,1152]{1,0:T(8,128)(2,1)} %dh_hbm.1, bf16[768,6144]{1,0:T(8,128)(2,1)} %tok_hbm.1, f32[1536,2,1152]{2,1,0:T(2,128)} %w_hbm.1), custom_call_target="tpu_custom_call" | custom-call | tf_op jit(solution)/shard_map/layer_exchange/pallas_call | solution.py:537
  66.5 9.9 %master_update.1 = (bf16[192,1152]{1,0:T(8,128)(2,1)}, f32[1536,2,1152]{2,1,0:T(2,128)}, f32[1536,2,1152]{2,1,0:T(2,128)}) custom-call(f32[24,128]{1,0:T(8,128)S(1)} %get-tuple-element.8.inv_ref, f32[2,1152]{1,0:T(2,128)S(1)} %get-tuple-element.9.cm_ref, bf16[1536,2304]{1,0:T(8,128)(2,1)S(1)} %get-tuple-element.10.grad_ref, ...), custom_call_target="tpu_custom_call" | custom-call | tf_op jit(solution)/shard_map/master_update/pallas_call | solution.py:590

commit v5 on v4

--- a/solution.py
+++ b/solution.py
@@ -143,7 +143,6 @@
             w_copies.append(
                 pltpu.make_async_copy(w_hbm.at[part, p, :], wv.at[p, part], w_sem.at[p, k])
             )
-            w_copies[-1].start()
     in_copies[1].start()
 
     barrier = pltpu.get_barrier_semaphore()
@@ -156,6 +155,8 @@
     ladder = jnp.where(before < after, 1.0, 0.0).astype(jnp.bfloat16)
     every = jnp.ones((LANE, LANE), jnp.bfloat16)
     in_copies[0].wait()
+    for copy in w_copies:
+        copy.start()
     named = jnp.logical_or(routes[0:1, :] == 0, routes[1:2, :] == 0)
     flag = jnp.where(named, 1.0, 0.0)
     mask = jnp.broadcast_to(flag, (16, toks)).astype(jnp.bfloat16)

time: 76.5 us -> 75.4 us (0.986)
  Pallas kernels: 75.7 us -> 74.6 us
    pallas_call x1, Pallas kernels: 65.8 us -> 64.8 us  [on_device(): pl.pallas_call(layer_kernel, name='layer_exchange', out_shape=(pltpu.VMEM...]
where the time goes in v5:
time: 75.4 us; the launch traced here: 75.2 us
  Pallas kernels  74.6 us (99%)
    pallas_call x1, Pallas kernels, on_device(): pl.pallas_call(layer_kernel, name='layer_exchange', out_shape=(pltpu.VMEM...  64.8 us
    pallas_call x1, Pallas kernels, on_device(): pl.pallas_call(update_kernel, name='master_update', out_shape=(jax.ShapeD...  9.85 us

profile of v5, /device:TPU:0, one launch (start us, length us, event | category | flops | bytes accessed | tf_op | source)
XLA Modules:
  0.0 75.2 jit_solution(8750503435142201664)
XLA Ops:
  0.6 64.8 %layer_exchange.1 = (bf16[192,1152]{1,0:T(8,128)(2,1)S(1)}, bf16[1536,2304]{1,0:T(8,128)(2,1)S(1)}, f32[2,1152]{1,0:T(2,128)S(1)}, f32[24,128]{1,0:T(8,128)S(1)}, f32[2,1536,1152]{2,1,0:T(8,128)S(1)}) custom-call(s32[2,768]{1,0:T(2,128)} %bitcast.1, bf16[192,1152]{1,0:T(8,128)(2,1)} %dh_hbm.1, bf16[768,6144]{1,0:T(8,128)(2,1)} %tok_hbm.1, f32[1536,2,1152]{2,1,0:T(2,128)} %w_hbm.1), custom_call_target="tpu_custom_call" | custom-call | tf_op jit(solution)/shard_map/layer_exchange/pallas_call | solution.py:538
  65.4 9.9 %master_update.1 = (bf16[192,1152]{1,0:T(8,128)(2,1)}, f32[1536,2,1152]{2,1,0:T(2,128)}, f32[1536,2,1152]{2,1,0:T(2,128)}) custom-call(f32[24,128]{1,0:T(8,128)S(1)} %get-tuple-element.8.inv_ref, f32[2,1152]{1,0:T(2,128)S(1)} %get-tuple-element.9.cm_ref, bf16[1536,2304]{1,0:T(8,128)(2,1)S(1)} %get-tuple-element.10.grad_ref, ...), custom_call_target="tpu_custom_call" | custom-call | tf_op jit(solution)/shard_map/master_update/pallas_call | solution.py:591

commit v6 on v5

--- a/solution.py
+++ b/solution.py
@@ -169,7 +169,6 @@
     place = jnp.concatenate(places, axis=1)[0:1, :].astype(jnp.int32)
     slot_id = lax.broadcasted_iota(jnp.int32, (slots, toks), 0)
     pick = jnp.where(slot_id == place, flag, 0.0).astype(jnp.bfloat16)
-    pl.semaphore_wait(barrier, len(greeted))
 
     def routed(h, jj, q):
         return sc.at[
@@ -190,6 +189,8 @@
         q_copies[n].wait()
         many = slots if n < 2 else sizes[0]
         qsend[n, 0:many] = jnp.dot(pick[0:many], tokq[n], preferred_element_type=jnp.float32).astype(jnp.bfloat16)
+        if n == 0:
+            pl.semaphore_wait(barrier, len(greeted))
         y_copy(0, n).start()
     def side_copies(h, jj):
         here = routed(h, jj, quarter_of)

time: 75.4 us -> 75.4 us (level)
  no operation moved by 1% of the time
where the time goes in v6:
time: 75.4 us; the launch traced here: 75.2 us
  Pallas kernels  74.6 us (99%)
    pallas_call x1, Pallas kernels, on_device(): pl.pallas_call(layer_kernel, name='layer_exchange', out_shape=(pltpu.VMEM...  64.7 us
    pallas_call x1, Pallas kernels, on_device(): pl.pallas_call(update_kernel, name='master_update', out_shape=(jax.ShapeD...  9.85 us

profile of v6, /device:TPU:0, one launch (start us, length us, event | category | flops | bytes accessed | tf_op | source)
XLA Modules:
  0.0 75.2 jit_solution(9281433627436148432)
XLA Ops:
  0.6 64.7 %layer_exchange.1 = (bf16[192,1152]{1,0:T(8,128)(2,1)S(1)}, bf16[1536,2304]{1,0:T(8,128)(2,1)S(1)}, f32[2,1152]{1,0:T(2,128)S(1)}, f32[24,128]{1,0:T(8,128)S(1)}, f32[2,1536,1152]{2,1,0:T(8,128)S(1)}) custom-call(s32[2,768]{1,0:T(2,128)} %bitcast.1, bf16[192,1152]{1,0:T(8,128)(2,1)} %dh_hbm.1, bf16[768,6144]{1,0:T(8,128)(2,1)} %tok_hbm.1, f32[1536,2,1152]{2,1,0:T(2,128)} %w_hbm.1), custom_call_target="tpu_custom_call" | custom-call | tf_op jit(solution)/shard_map/layer_exchange/pallas_call | solution.py:539
  65.4 9.9 %master_update.1 = (bf16[192,1152]{1,0:T(8,128)(2,1)}, f32[1536,2,1152]{2,1,0:T(2,128)}, f32[1536,2,1152]{2,1,0:T(2,128)}) custom-call(f32[24,128]{1,0:T(8,128)S(1)} %get-tuple-element.8.inv_ref, f32[2,1152]{1,0:T(2,128)S(1)} %get-tuple-element.9.cm_ref, bf16[1536,2304]{1,0:T(8,128)(2,1)S(1)} %get-tuple-element.10.grad_ref, ...), custom_call_target="tpu_custom_call" | custom-call | tf_op jit(solution)/shard_map/master_update/pallas_call | solution.py:592
